TPU v7x, 512 devices: a whole 4x8x8 slice. The times are simulated.
512 devices in a mesh: grp: 32 (over x, z), exp: 16 (over y, core).
Axes of the slice: x: 4, y: 8, z: 8, core: 2. Of those that a mesh axis runs over, the one named last changes fastest.
Arguments:
- step_inputs: bfloat16 [32, 4, 4, 2048], P('grp'), may hold values from -10 to 10
- parents: int32 [32, 4, 4], P('grp'), may hold values from 0 to 7
- routes: int32 [32, 4, 4, 6], P('grp'), may hold values from 0 to 63, all different within a row; in each aligned block of 16 rows (0 to 15, 16 to 31, ..., all dimensions but the last counted through in order) at most 3 rows name the same one
- w_qkv: bfloat16 [2048, 3, 2048], P(None, None, 'exp'), may hold values from -0.125 to 0.125
- w_out: bfloat16 [2048, 2048], P('exp'), may hold values from -0.125 to 0.125
- prompt_keys: bfloat16 [32, 1024, 2048], P('grp', None, 'exp'), may hold values from -128 to 128, as said below
- prompt_values: bfloat16 [32, 1024, 2048], P('grp', None, 'exp'), may hold values from -6 to 6
- prompt_parts: int32 [32], P('grp'), may hold values from 1 to 1024, as said below
- tail_keys: bfloat16 [32, 4, 60, 2048], P('grp', None, None, 'exp'), may hold values from -18 to 18
- tail_values: bfloat16 [32, 4, 60, 2048], P('grp', None, None, 'exp'), may hold values from -6 to 6
- w_router: bfloat16 [2048, 64], P('exp'), may hold values from -0.022097087 to 0.022097087
- norm_gain: float32 [2048], P('exp'), may hold values from 0.1 to 1.9
- w_gate_up: bfloat16 [64, 2048, 2816], P('grp', 'exp'), may hold values from -0.125 to 0.125
- w_down: bfloat16 [64, 2048, 1408], P('grp', 'exp'), may hold values from -0.15625 to 0.15625
Outputs:
- layer_out: bfloat16 [32, 4, 4, 2048], P('grp', None, None, 'exp')
Inputs may be any that keep to these rules, and one draw needn't show every extreme that they name: `prompt_keys`: keys of order a few units. `prompt_parts`: each part holds 1 to 1024 valid positions; in every draw some part holds exactly 1024. `routes`: within the rows of one slot no expert is named more than 3 times, and in every draw some expert is named exactly 3 times by the rows of some slot.
All inputs are finite; a program needn't handle non-finite values.
Results may differ from a plain program's by a relative error of at most 0.013.
Values may be sent and summed in bfloat16 or wider, within the bound.
A program may use at most 64 MiB of HBM per device.

v0:
```python
import jax
import jax.numpy as jnp
from jax import lax
from jax.sharding import PartitionSpec as P

D = 2048
HDIM = 128
EXPERTS = 64
FFE = 1408
TOPK = 6
BEAMS = 8
STEPS = 4
TAIL = 64
CAP = 1024
CAP_E = 3
HALF = 4
PREV = 60


NEGATIVE = -1e30
EPSILON = 1e-06


def swapped(value, axis, stride):
    mask = 2**stride
    pairs = [(source, source ^ mask) for source in range(lax.axis_size(axis))]
    return lax.ppermute(value, axis, pairs)


def ordered(low_first, own_part, other_part):
    return jnp.concatenate(
        [jnp.where(low_first, own_part, other_part), jnp.where(low_first, other_part, own_part)],
        axis=0,
    )


def on_device(
    step_inputs,
    parents,
    routes,
    w_qkv,
    w_out,
    prompt_keys,
    prompt_values,
    prompt_parts,
    tail_keys,
    tail_values,
    w_router,
    norm_gain,
    w_gate_up,
    w_down,
):
    pair_half = lax.axis_index("grp") % 2
    column = lax.axis_index("exp")
    low_first = pair_half == 0
    own_inputs = step_inputs[0]
    own_parents = parents[0]
    other_inputs, other_parents = swapped((own_inputs, own_parents), "grp", 0)
    inputs_all = jnp.concatenate(
        [
            jnp.where(low_first, own_inputs, other_inputs),
            jnp.where(low_first, other_inputs, own_inputs),
        ],
        axis=1,
    )
    local_width = w_qkv.shape[2]
    local_heads = local_width // HDIM
    packed = jnp.dot(
        inputs_all.reshape(STEPS * BEAMS, D),
        w_qkv.reshape(D, 3 * local_width),
        preferred_element_type=jnp.float32,
    )
    packed = packed.astype(jnp.bfloat16).reshape(STEPS, BEAMS, 3, local_heads, HDIM)
    query_all = packed[:, :, 0]
    key_new = packed[:, :, 1]
    value_new = packed[:, :, 2]
    score_scale = HDIM ** (-0.5)
    own_start = pair_half * HALF
    other_start = (1 - pair_half) * HALF
    keys_here = prompt_keys[0].reshape(CAP, local_heads, HDIM)
    values_here = prompt_values[0].reshape(CAP, local_heads, HDIM)
    live_pos = jnp.arange(CAP, dtype=jnp.int32) < prompt_parts[0]
    prompt_scores = (
        jnp.einsum("sbhd,nhd->sbhn", query_all, keys_here, preferred_element_type=jnp.float32)
        * score_scale
    )
    prompt_scores = jnp.where(live_pos, prompt_scores, NEGATIVE)
    prompt_top = jnp.max(prompt_scores, axis=3)
    prompt_weights = jnp.exp(prompt_scores - prompt_top[..., None])
    prompt_total = jnp.sum(prompt_weights, axis=3)
    prompt_mix = jnp.einsum(
        "sbhn,nhd->sbhd",
        prompt_weights,
        values_here.astype(jnp.float32),
        precision=lax.Precision.HIGHEST,
    )

    def take_beams(array, start):
        return lax.dynamic_slice_in_dim(array, start, HALF, 1)

    far_top, far_total, far_mix = swapped(
        (
            take_beams(prompt_top, other_start),
            take_beams(prompt_total, other_start),
            take_beams(prompt_mix, other_start),
        ),
        "grp",
        0,
    )
    own_ids = own_start + jnp.arange(HALF, dtype=jnp.int32)
    keys_flat = key_new.reshape(STEPS, BEAMS, local_width)
    values_flat = value_new.reshape(STEPS, BEAMS, local_width)
    step_keys = []
    step_values = []
    tail_k = jnp.pad(tail_keys[0], ((0, 0), (0, STEPS), (0, 0)))
    tail_v = jnp.pad(tail_values[0], ((0, 0), (0, STEPS), (0, 0)))
    for step_index in range(STEPS):
        far_k, far_v = swapped((tail_k, tail_v), "grp", 0)
        every_k = ordered(low_first, tail_k, far_k)
        every_v = ordered(low_first, tail_v, far_v)
        chosen = own_parents[step_index]
        tail_k = every_k[chosen].at[:, PREV + step_index].set(keys_flat[step_index][own_ids])
        tail_v = every_v[chosen].at[:, PREV + step_index].set(values_flat[step_index][own_ids])
        step_keys.append(tail_k)
        step_values.append(tail_v)
    tail_k_all = jnp.stack(step_keys).reshape(STEPS, HALF, TAIL, local_heads, HDIM)
    tail_v_all = jnp.stack(step_values).reshape(STEPS, HALF, TAIL, local_heads, HDIM)
    own_query = take_beams(query_all, own_start)
    tail_scores = (
        jnp.einsum("sbhd,sbnhd->sbhn", own_query, tail_k_all, preferred_element_type=jnp.float32)
        * score_scale
    )
    tail_live = (
        jnp.arange(TAIL, dtype=jnp.int32)[None, :]
        <= PREV + jnp.arange(STEPS, dtype=jnp.int32)[:, None]
    )
    tail_scores = jnp.where(tail_live[:, None, None, :], tail_scores, NEGATIVE)
    tail_top = jnp.max(tail_scores, axis=3)
    tail_weights = jnp.exp(tail_scores - tail_top[..., None])
    tail_total = jnp.sum(tail_weights, axis=3)
    tail_mix = jnp.einsum(
        "sbhn,sbnhd->sbhd",
        tail_weights,
        tail_v_all.astype(jnp.float32),
        precision=lax.Precision.HIGHEST,
    )
    near_top = take_beams(prompt_top, own_start)
    near_total = take_beams(prompt_total, own_start)
    near_mix = take_beams(prompt_mix, own_start)
    best_top = jnp.maximum(jnp.maximum(near_top, tail_top), far_top)
    near_factor = jnp.exp(near_top - best_top)
    tail_factor = jnp.exp(tail_top - best_top)
    far_factor = jnp.exp(far_top - best_top)
    whole_total = near_total * near_factor + tail_total * tail_factor + far_total * far_factor
    whole_mix = (
        near_mix * near_factor[..., None]
        + tail_mix * tail_factor[..., None]
        + far_mix * far_factor[..., None]
    )
    row_count = STEPS * HALF
    attention = (
        (whole_mix / whole_total[..., None]).astype(jnp.bfloat16).reshape(row_count, local_width)
    )
    proj_terms = jnp.dot(attention, w_out, preferred_element_type=jnp.float32)
    attn_proj = lax.psum_scatter(proj_terms, "exp", scatter_dimension=1, tiled=True)
    feature_count = attn_proj.shape[1]
    residual_in = lax.dynamic_slice_in_dim(
        own_inputs.reshape(row_count, D), column * feature_count, feature_count, 1
    ).astype(jnp.float32)
    residual_rows = residual_in + attn_proj
    square_total = lax.psum(jnp.sum(residual_rows * residual_rows, axis=1), "exp")
    normed = (residual_rows * lax.rsqrt(square_total[:, None] / D + EPSILON) * norm_gain).astype(
        jnp.bfloat16
    )
    logits = lax.psum(jnp.dot(normed, w_router, preferred_element_type=jnp.float32), "exp")
    probs = jax.nn.softmax(logits, axis=1)
    chosen_routes = routes[0].reshape(row_count, TOPK)
    route_match = chosen_routes[:, :, None] == jnp.arange(EXPERTS, dtype=jnp.int32)[None, None, :]
    picked = jnp.sum(jnp.where(route_match, probs[:, None, :], 0.0), axis=2)
    route_share = picked / jnp.sum(picked, axis=1, keepdims=True)
    flat_match = route_match.reshape(row_count * TOPK, EXPERTS).astype(jnp.int32)
    earlier = jnp.cumsum(flat_match, axis=0) - flat_match
    slot_rank = jnp.sum(flat_match * earlier, axis=1)
    target = chosen_routes.reshape(row_count * TOPK) * CAP_E + slot_rank
    slot_place = target[:, None] == jnp.arange(EXPERTS * CAP_E, dtype=jnp.int32)[None, :]
    token_place = jnp.sum(
        slot_place.reshape(row_count, TOPK, EXPERTS * CAP_E).astype(jnp.float32), axis=1
    ).astype(jnp.bfloat16)
    share_matrix = jnp.sum(
        (slot_place.astype(jnp.float32) * route_share.reshape(row_count * TOPK)[:, None]).reshape(
            row_count, TOPK, EXPERTS * CAP_E
        ),
        axis=1,
    )
    outgoing = jnp.dot(token_place.T, normed, preferred_element_type=jnp.float32).astype(
        jnp.bfloat16
    )
    incoming = lax.all_to_all(outgoing, "grp", split_axis=0, concat_axis=0, tiled=True)
    groups = lax.axis_size("grp")
    local_experts = w_gate_up.shape[0]
    expert_input = incoming.reshape(groups, local_experts, CAP_E, feature_count)
    partial_units = jnp.einsum(
        "slcd,ldf->slcf", expert_input, w_gate_up, preferred_element_type=jnp.float32
    )
    summed_units = lax.psum(partial_units.astype(jnp.bfloat16), "exp").astype(jnp.float32)
    hidden_units = (jax.nn.silu(summed_units[..., :FFE]) * summed_units[..., FFE:]).astype(
        jnp.bfloat16
    )
    expert_result = jnp.einsum(
        "slcf,ldf->slcd", hidden_units, w_down, preferred_element_type=jnp.float32
    ).astype(jnp.bfloat16)
    returned = lax.all_to_all(
        expert_result.reshape(groups * local_experts * CAP_E, feature_count),
        "grp",
        split_axis=0,
        concat_axis=0,
        tiled=True,
    )
    expert_mix = jnp.dot(
        share_matrix, returned.astype(jnp.float32), precision=lax.Precision.HIGHEST
    )
    return (residual_rows + expert_mix).astype(jnp.bfloat16).reshape(1, STEPS, HALF, feature_count)


def solution(mesh):
    placed = (
        P("grp", None, None, None),
        P("grp", None, None),
        P("grp", None, None, None),
        P(None, None, "exp"),
        P("exp", None),
        P("grp", None, "exp"),
        P("grp", None, "exp"),
        P("grp"),
        P("grp", None, None, "exp"),
        P("grp", None, None, "exp"),
        P("exp", None),
        P("exp"),
        P("grp", "exp", None),
        P("grp", "exp", None),
    )
    return jax.shard_map(
        on_device,
        mesh=mesh,
        in_specs=placed,
        out_specs=P("grp", None, None, "exp"),
        check_vma=False,
    )
```

profile of v0, /device:TPU:1, one launch (start us, length us, event | category | flops | bytes accessed | tf_op | source)
XLA Modules:
  0.0 347.8 jit_solution(5062878199130492356)
XLA Ops:
  6.5 1.0 copy.96
  7.5 4.8 %collective-permute-start.6 = (bf16[4,64,128]{2,1,0:T(8,128)(2,1)S(1)}, bf16[4,64,128]{2,1,0:T(8,128)(2,1)S(1)}, u32[]{:S(2)}, u32[]{:S(2)}) collective-permute-start(bf16[4,64,128]{2,1,0:T(8,128)(2,1)S(1)} %pad.24), channel_id=1, source_target_pairs={{0,16},{16,0},{32,48},{48,32},{64,80},{80,64},{96,112},{112,96},{1... | collective-permute-start | bytes 196616 | tf_op jit(solution)/shard_map/ppermute | solution.py:27
  12.4 0.8 copy.97
  13.2 0.6 pad.23
  13.8 1.9 collective-permute-start.1
  15.7 3.4 collective-permute-start
  19.8 0.8 eq.43
  20.6 0.6 iota_compare_fusion.4
  21.2 0.8 fusion.57
  22.1 0.6 pad_clamp_fusion.4
  22.8 0.7 reduce_window_sum.11
  23.5 1.8 copy.61
  25.3 0.6 iota_compare_fusion.3
  25.9 1.3 gather_fusion.8
  27.2 0.9 broadcast_select_fusion.15
  28.2 0.7 gather_fusion
  28.9 0.9 broadcast_select_fusion.17
  29.8 0.6 convolution_convert_fusion.3
  30.4 0.6 gather_fusion.15
  31.0 0.6 gather_fusion.13
  31.5 0.6 gather_fusion.11
  32.1 0.6 gather_fusion.9
  32.7 0.6 gather_fusion.7
  33.2 0.6 gather_fusion.5
  33.8 0.6 gather_fusion.3
  34.4 0.6 gather_fusion.1
  35.0 1.9 collective-permute-start.2
  36.9 1.3 scatter.34
  38.2 3.3 collective-permute-start.7
  41.6 0.3 fusion.64
  42.1 1.3 fusion.25
  43.5 1.9 collective-permute-start.5
  45.4 3.4 collective-permute-start.11
  48.8 1.9 collective-permute-start.10
  50.8 0.6 gather_fusion.2
  51.4 3.4 collective-permute-start.3
  54.8 0.9 broadcast_select_fusion.5
  55.7 0.6 gather_fusion.10
  56.3 1.9 collective-permute-start.8
  58.3 0.6 gather_fusion.4
  58.9 3.4 collective-permute-start.4
  62.3 0.6 gather_fusion.12
  62.9 1.9 collective-permute-start.9
  64.9 0.6 gather_fusion.6
  65.5 0.2 fusion.9
  66.1 2.8 collective-permute-done.9
  68.9 0.6 gather_fusion.14
  69.5 1.2 fusion.17
  70.9 0.8 fusion.65
  72.3 63.2 %reduce-scatter.2.cloned.1.call-done = f32[16,128]{1,0:T(8,128)} async-done(((f32[16,2048]{1,0:T(8,128)}), f32[16,128]{1,0:T(8,128)}) %reduce-scatter.2.cloned.1.call-update) | async-done | bytes 8208 | tf_op jit(solution)/shard_map/reduce_scatter | solution.py:165
  135.5 0.8 multiply_reduce_fusion
  136.3 25.2 %psum.21 = f32[16]{0:T(128)S(1)} all-reduce(f32[16]{0:T(128)S(1)} %multiply_reduce_fusion), channel_id=1, replica_groups=mesh['grp'=32,'exp'=16] {'exp'}, use_global_device_ids=true, to_apply=%region_8.9 | all-reduce | flops 16 | bytes 128 | tf_op jit(solution)/shard_map/psum | solution.py:171
  161.6 0.8 multiply_convert_fusion
  162.5 25.3 %psum.22 = f32[16,64]{1,0:T(8,128)S(1)} all-reduce(f32[16,64]{1,0:T(8,128)S(1)} %fusion.66), channel_id=1, replica_groups=mesh['grp'=32,'exp'=16] {'exp'}, use_global_device_ids=true, to_apply=%region_9.10 | all-reduce | flops 1024 | bytes 8192 | tf_op jit(solution)/shard_map/psum | solution.py:175
  187.9 0.2 fusion.43
  188.1 0.2 select_reduce_fusion.1
  188.5 0.2 convolution_convert_fusion.2
  188.7 17.6 %all_to_all.21 = bf16[32,6,128]{2,1,0:T(8,128)(2,1)S(1)} all-to-all(bf16[32,6,128]{2,1,0:T(8,128)(2,1)S(1)} %all_to_all.14), channel_id=1, replica_groups=mesh['grp'=32,'exp'=16] {'grp'}, dimensions={0} | all-to-all | bytes 98304 | tf_op jit(solution)/shard_map/all_to_all | solution.py:198
  206.3 1.5 fusion
  207.8 111.8 %all-reduce.4.cloned.1.call-done = bf16[32,2,3,2816]{3,0,2,1:T(8,128)(2,1)} async-done(((bf16[32,2,3,2816]{3,0,2,1:T(8,128)(2,1)}), bf16[32,2,3,2816]{3,0,2,1:T(8,128)(2,1)}) %all-reduce.4.cloned.1.call-update) | async-done | bytes 1081360 | tf_op jit(solution)/shard_map/psum | solution.py:205
  319.7 1.4 convert_element_type.62
  321.1 0.4 convolution_convert_fusion.1
  321.6 18.6 %all_to_all.22 = bf16[32,6,128]{2,1,0:T(8,128)(2,1)S(1)} all-to-all(bf16[32,6,128]{2,1,0:T(8,128)(2,1)S(1)} %copy.84), channel_id=1, replica_groups=mesh['grp'=32,'exp'=16] {'grp'}, dimensions={0} | all-to-all | bytes 98304 | tf_op jit(solution)/shard_map/all_to_all | solution.py:212
  340.2 0.8 fusion.5
  (111 shorter events, 2.7 us)
Async XLA Ops:
  6.5 199.8 %copy-start = (bf16[2,128,2816]{2,1,0:T(8,128)(2,1)S(1)}, bf16[2,128,2816]{2,1,0:T(8,128)(2,1)}, u32[]{:S(2)}) copy-start(bf16[2,128,2816]{2,1,0:T(8,128)(2,1)} %param.42) | copy-start | bytes 4325380
  6.5 129.0 %reduce-scatter.2.cloned.1.call-start = ((), (), s32[]{:S(2)}) async-start(), calls=%async_computation.3 | async-start | bytes 139264 | tf_op jit(solution)/shard_map/reduce_scatter | solution.py:165
  7.5 18.3 %collective-permute-start.6 = (bf16[4,64,128]{2,1,0:T(8,128)(2,1)S(1)}, bf16[4,64,128]{2,1,0:T(8,128)(2,1)S(1)}, u32[]{:S(2)}, u32[]{:S(2)}) collective-permute-start(bf16[4,64,128]{2,1,0:T(8,128)(2,1)S(1)} %pad.24), channel_id=1, source_target_pairs={{0,16},{16,0},{32,48},{48,32},{64,80},{80,64},{96,112},{112,96},{1... | collective-permute-start | bytes 196616 | tf_op jit(solution)/shard_map/ppermute | solution.py:27
  13.8 13.4 %collective-permute-start.1 = (bf16[4,64,128]{2,1,0:T(8,128)(2,1)}, bf16[4,64,128]{2,1,0:T(8,128)(2,1)}, u32[]{:S(2)}, u32[]{:S(2)}) collective-permute-start(bf16[4,64,128]{2,1,0:T(8,128)(2,1)} %pad.23), channel_id=1, source_target_pairs={{0,16},{16,0},{32,48},{48,32},{64,80},{80,64},{96,112},{112,96},{1... | collective-permute-start | bytes 196616 | tf_op jit(solution)/shard_map/ppermute | solution.py:27
  15.7 13.1 %collective-permute-start = (bf16[4,4,2048]{2,1,0:T(4,128)(2,1)}, bf16[4,4,2048]{2,1,0:T(4,128)(2,1)}, u32[]{:S(2)}, u32[]{:S(2)}) collective-permute-start(bf16[4,4,2048]{2,1,0:T(4,128)(2,1)} %bitcast.229), channel_id=1, source_target_pairs={{0,16},{16,0},{32,48},{48,32},{64,80},{80,64},{96,112},{112,96},{1... | collective-permute-start | bytes 196616 | tf_op jit(solution)/shard_map/ppermute | solution.py:27
  20.6 2.2 copy-start.10
  23.5 5.4 %copy-start.3 = (bf16[1,4,4,2048]{3,2,1,0:T(4,128)(2,1)S(1)}, bf16[1,4,4,2048]{3,2,1,0:T(4,128)(2,1)}, u32[]{:S(2)}) copy-start(bf16[1,4,4,2048]{3,2,1,0:T(4,128)(2,1)} %param.30) | copy-start | bytes 196612
  27.2 14.4 %copy-start.2 = (bf16[1,1024,128]{2,1,0:T(8,128)(2,1)S(1)}, bf16[1,1024,128]{2,1,0:T(8,128)(2,1)}, u32[]{:S(2)}) copy-start(bf16[1,1024,128]{2,1,0:T(8,128)(2,1)} %param.35) | copy-start | bytes 786436
  28.9 12.8 %copy-start.13 = (pred[1024]{0:T(1024)(128)(4,1)S(1)}, pred[1024]{0:T(1024)(128)(4,1)}, u32[]{:S(2)}) copy-start(pred[1024]{0:T(1024)(128)(4,1)} %iota_compare_fusion.3) | copy-start | bytes 3076
  35.0 15.8 %copy-start.4 = (bf16[4,64,128]{2,1,0:T(8,128)(2,1)}, bf16[4,64,128]{2,1,0:T(8,128)(2,1)S(1)}, u32[]{:S(2)}) copy-start(bf16[4,64,128]{2,1,0:T(8,128)(2,1)S(1)} %scatter.26) | copy-start | bytes 196612
  35.0 15.7 %collective-permute-start.2 = (bf16[4,64,128]{2,1,0:T(8,128)(2,1)S(1)}, bf16[4,64,128]{2,1,0:T(8,128)(2,1)S(1)}, u32[]{:S(2)}, u32[]{:S(2)}) collective-permute-start(bf16[4,64,128]{2,1,0:T(8,128)(2,1)S(1)} %scatter.26), channel_id=1, source_target_pairs={{0,16},{16,0},{32,48},{48,32},{64,80},{80,64},{96,112},{112,96},{1... | collective-permute-start | bytes 196616 | tf_op jit(solution)/shard_map/ppermute | solution.py:27
  38.2 16.5 %collective-permute-start.7 = (bf16[4,64,128]{2,1,0:T(8,128)(2,1)}, bf16[4,64,128]{2,1,0:T(8,128)(2,1)S(1)}, u32[]{:S(2)}, u32[]{:S(2)}) collective-permute-start(bf16[4,64,128]{2,1,0:T(8,128)(2,1)} %scatter.34), channel_id=1, source_target_pairs={{0,16},{16,0},{32,48},{48,32},{64,80},{80,64},{96,112},{112,96},{1... | collective-permute-start | bytes 196616 | tf_op jit(solution)/shard_map/ppermute | solution.py:27
  43.5 27.1 %collective-permute-start.5 = (f32[4,4,1]{1,0,2:T(4,128)S(1)}, f32[4,4,1]{1,0,2:T(4,128)S(1)}, u32[]{:S(2)}, u32[]{:S(2)}) collective-permute-start(f32[4,4,1]{1,0,2:T(4,128)S(1)} %dynamic-slice_bitcast_fusion.3), channel_id=1, source_target_pairs={{0,16},{16,0},{32,48},{48,32},{64,80},{80,64},{96,112},{112,96},{1... | collective-permute-start | bytes 200 | tf_op jit(solution)/shard_map/ppermute | solution.py:27
  45.4 25.3 %collective-permute-start.11 = (f32[4,4,1]{1,0,2:T(4,128)S(1)}, f32[4,4,1]{1,0,2:T(4,128)S(1)}, u32[]{:S(2)}, u32[]{:S(2)}) collective-permute-start(f32[4,4,1]{1,0,2:T(4,128)S(1)} %dynamic-slice_bitcast_fusion.2), channel_id=1, source_target_pairs={{0,16},{16,0},{32,48},{48,32},{64,80},{80,64},{96,112},{112,96},{1... | collective-permute-start | bytes 200 | tf_op jit(solution)/shard_map/ppermute | solution.py:27
  48.8 22.0 %collective-permute-start.10 = (f32[4,4,1,128]{3,1,0,2:T(4,128)S(1)}, f32[4,4,1,128]{3,1,0,2:T(4,128)S(1)}, u32[]{:S(2)}, u32[]{:S(2)}) collective-permute-start(f32[4,4,1,128]{3,1,0,2:T(4,128)S(1)} %dynamic-slice_bitcast_fusion), channel_id=1, source_target_pairs={{0,16},{16,0},{32,48},{48,32},{64,80},{80,64},{96,112},{112,96},{1... | collective-permute-start | bytes 24584 | tf_op jit(solution)/shard_map/ppermute | solution.py:27
  50.8 14.7 %copy-start.5 = (bf16[4,64,128]{2,1,0:T(8,128)(2,1)S(1)}, bf16[4,64,128]{2,1,0:T(8,128)(2,1)}, u32[]{:S(2)}) copy-start(bf16[4,64,128]{2,1,0:T(8,128)(2,1)} %copy-done.4) | copy-start | bytes 196612
  51.4 6.8 %collective-permute-start.3 = (bf16[4,64,128]{2,1,0:T(8,128)(2,1)S(1)}, bf16[4,64,128]{2,1,0:T(8,128)(2,1)S(1)}, u32[]{:S(2)}, u32[]{:S(2)}) collective-permute-start(bf16[4,64,128]{2,1,0:T(8,128)(2,1)S(1)} %scatter.29), channel_id=1, source_target_pairs={{0,16},{16,0},{32,48},{48,32},{64,80},{80,64},{96,112},{112,96},{1... | collective-permute-start | bytes 196616 | tf_op jit(solution)/shard_map/ppermute | solution.py:27
  56.3 9.5 %copy-start.12 = (pred[4,64]{1,0:T(4,128)(4,1)S(1)}, pred[4,64]{1,0:T(4,128)(4,1)}, u32[]{:S(2)}) copy-start(pred[4,64]{1,0:T(4,128)(4,1)} %iota_compare_fusion.4) | copy-start | bytes 772
  56.3 6.0 %collective-permute-start.8 = (bf16[4,64,128]{2,1,0:T(8,128)(2,1)S(1)}, bf16[4,64,128]{2,1,0:T(8,128)(2,1)S(1)}, u32[]{:S(2)}, u32[]{:S(2)}) collective-permute-start(bf16[4,64,128]{2,1,0:T(8,128)(2,1)S(1)} %scatter.35), channel_id=1, source_target_pairs={{0,16},{16,0},{32,48},{48,32},{64,80},{80,64},{96,112},{112,96},{1... | collective-permute-start | bytes 196616 | tf_op jit(solution)/shard_map/ppermute | solution.py:27
  58.9 6.0 %collective-permute-start.4 = (bf16[4,64,128]{2,1,0:T(8,128)(2,1)S(1)}, bf16[4,64,128]{2,1,0:T(8,128)(2,1)S(1)}, u32[]{:S(2)}, u32[]{:S(2)}) collective-permute-start(bf16[4,64,128]{2,1,0:T(8,128)(2,1)S(1)} %scatter.30), channel_id=1, source_target_pairs={{0,16},{16,0},{32,48},{48,32},{64,80},{80,64},{96,112},{112,96},{1... | collective-permute-start | bytes 196616 | tf_op jit(solution)/shard_map/ppermute | solution.py:27
  62.9 5.9 %collective-permute-start.9 = (bf16[4,64,128]{2,1,0:T(8,128)(2,1)S(1)}, bf16[4,64,128]{2,1,0:T(8,128)(2,1)S(1)}, u32[]{:S(2)}, u32[]{:S(2)}) collective-permute-start(bf16[4,64,128]{2,1,0:T(8,128)(2,1)S(1)} %scatter.36), channel_id=1, source_target_pairs={{0,16},{16,0},{32,48},{48,32},{64,80},{80,64},{96,112},{112,96},{1... | collective-permute-start | bytes 196616 | tf_op jit(solution)/shard_map/ppermute | solution.py:27
  64.9 6.1 %copy-start.1 = (bf16[128,2048]{1,0:T(8,128)(2,1)S(1)}, bf16[128,2048]{1,0:T(8,128)(2,1)}, u32[]{:S(2)}) copy-start(bf16[128,2048]{1,0:T(8,128)(2,1)} %param.34) | copy-start | bytes 1572868
  65.8 6.1 %copy-start.6 = (s32[96,64]{1,0:T(8,128)S(1)}, s32[96,64]{1,0:T(8,128)}, u32[]{:S(2)}) copy-start(s32[96,64]{1,0:T(8,128)} %reduce_window_sum.11) | copy-start | bytes 73732
  65.8 6.1 %copy-start.11 = (s32[96]{0:T(128)S(1)}, s32[96]{0:T(128)}, u32[]{:S(2)}) copy-start(s32[96]{0:T(128)} %copy-done.10) | copy-start | bytes 1156
  65.8 6.3 %copy-start.7 = (s32[1,4,4,6]{3,2,1,0:T(4,128)S(1)}, s32[1,4,4,6]{3,2,1,0:T(4,128)}, u32[]{:S(2)}) copy-start(s32[1,4,4,6]{3,2,1,0:T(4,128)} %param.32) | copy-start | bytes 1156
  65.8 95.8 %copy-start.14 = (f32[128]{0:T(128)S(1)}, f32[128]{0:T(128)}, u32[]{:S(2)}) copy-start(f32[128]{0:T(128)} %param.41) | copy-start | bytes 1540
  65.8 96.6 %copy-start.9 = (bf16[128,64]{0,1:T(8,128)(2,1)S(1)}, bf16[128,64]{0,1:T(8,128)(2,1)}, u32[]{:S(2)}) copy-start(bf16[128,64]{0,1:T(8,128)(2,1)} %param.40) | copy-start | bytes 49156
  71.8 247.9 %all-reduce.4.cloned.1.call-start = ((), (), s32[]{:S(2)}) async-start(), calls=%async_computation.4 | async-start | bytes 2162688 | tf_op jit(solution)/shard_map/psum | solution.py:205
  207.8 113.3 %copy-start.15 = (bf16[2,128,1408]{2,1,0:T(8,128)(2,1)S(1)}, bf16[2,128,1408]{2,1,0:T(8,128)(2,1)}, u32[]{:S(2)}) copy-start(bf16[2,128,1408]{2,1,0:T(8,128)(2,1)} %param.43) | copy-start | bytes 2162692
  321.1 19.1 %copy-start.8 = (f32[16,128]{1,0:T(8,128)S(1)}, f32[16,128]{1,0:T(8,128)}, u32[]{:S(2)}) copy-start(f32[16,128]{1,0:T(8,128)} %reduce-scatter.2.cloned.1.call-done) | copy-start | bytes 24580
Sparse Core Ops, SparseCore 0:
  71.9 63.5 reduce-scatter.1
  207.9 111.6 all-reduce.3
where the time goes:
time: 350 us; the launch traced here: 348 us
  waiting for transfers between devices  178 us (51%)
  blocking collectives  86.7 us (25%)
  starting transfers between devices  33.2 us (9%)
  local copies, waits for them, and re-layouts  17 us (5%)
  between operations  14.8 us (4%)
  other arithmetic  10.9 us (3%)
  matrix products  7.32 us (2%)
    psum x1, waiting for transfers between devices, on_device(): lax.psum(partial_units.astype(jnp.bfloat16), 'exp').astype(jnp.float32)  112 us
    reduce_scatter x1, waiting for transfers between devices, on_device(): lax.psum_scatter(proj_terms, 'exp', scatter_dimension=1, tiled=True)  63.2 us
    ppermute x12, starting transfers between devices, swapped(): return lax.ppermute(value, axis, pairs)  33.1 us
    psum x1, blocking collectives, on_device(): lax.psum(jnp.dot(normed, w_router, preferred_element_type=jnp.float32), '...  25.3 us
    psum x1, blocking collectives, on_device(): lax.psum(jnp.sum(residual_rows * residual_rows, axis=1), 'exp')  25.2 us
    all_to_all x1, blocking collectives, on_device(): lax.all_to_all(expert_result.reshape(groups * local_experts * CAP_E, feat...  18.6 us
    all_to_all x1, blocking collectives, on_device(): lax.all_to_all(outgoing, 'grp', split_axis=0, concat_axis=0, tiled=True)  17.6 us
  transfers between devices with their start and end apart: 14, of which 3 were waited for; matrix products, arithmetic and copies ran while one was open for 6% of the time, Pallas kernels for 0%

commit v1 on v0

v1 whole, which is shorter than its diff:
```python
import functools

import jax
import jax.numpy as jnp
from jax import lax
from jax.experimental import pallas as pl
from jax.experimental.pallas import tpu as pltpu
from jax.sharding import PartitionSpec as P

HDIM = 128
TOPK = 6
STEPS = 4
HALF = 4
ROWS = STEPS * HALF
CAP_E = 3
PREV = 60
TAILP = 64
SEND = 8
BLOCK = 12
PADB = 16

NEGATIVE = -1e30
EPSILON = 1e-06
F32 = jnp.float32
BF16 = jnp.bfloat16


def iota(shape, axis):
    return lax.broadcasted_iota(jnp.int32, shape, axis)


def dot(a, b, precision=None):
    return jnp.dot(a, b, preferred_element_type=F32, precision=precision)


def dot_t(a, b, precision=None):
    return lax.dot_general(
        a, b, (((1,), (1,)), ((), ())), preferred_element_type=F32, precision=precision
    )


def one_hot(cond):
    return jnp.where(cond, 1.0, 0.0).astype(BF16)


def split_high(value):
    high = value.astype(BF16)
    return high, (value - high.astype(F32)).astype(BF16)


def kernel(
    groups,
    columns,
    topk,
    x_ref,
    par_ref,
    routes_ref,
    parts_ref,
    gain_in,
    wr_in,
    wqkv_hbm,
    wout_hbm,
    pk_hbm,
    pv_hbm,
    tk_ref,
    tv_ref,
    wgu_hbm,
    wd_hbm,
    out_ref,
    xs,
    rts,
    gain,
    wr,
    wqkv,
    wout,
    kall,
    vall,
    wgu,
    wd,
    qkv,
    part_send,
    part_recv,
    proj_send,
    proj_recv,
    stat_send,
    stat_recv,
    disp_send,
    disp_recv,
    sq_send,
    sq_recv,
    gu_send,
    gu_recv,
    gsum,
    hid,
    ret_send,
    ret_recv,
    mix_send,
    mix_recv,
    local_sem,
    send_sem,
    recv_sem,
):
    chips = columns // 2
    ffe = wd.shape[1]
    cap = pk_hbm.shape[1]
    experts = wr.shape[1]
    depth = x_ref.shape[3]
    g = lax.axis_index("grp")
    e = lax.axis_index("exp")
    y = e // 2
    c = e % 2
    half = g % 2
    partner = g + 1 - 2 * half
    sibling = e + 1 - 2 * c
    own_rows = pl.ds(pl.multiple_of(c * HDIM, HDIM), HDIM)

    def local(src, dst, index):
        copy = pltpu.make_async_copy(src, dst, local_sem.at[index])
        copy.start()
        return copy

    def remote(src, dst, index, **where):
        return pltpu.make_async_remote_copy(
            src_ref=src,
            dst_ref=dst,
            send_sem=send_sem.at[index],
            recv_sem=recv_sem.at[index],
            device_id=where,
            device_id_type=pl.DeviceIdType.MESH,
        )

    def wait_bytes(ref, sem):
        pltpu.make_async_copy(ref, ref, sem).wait()

    load_qkv = local(wqkv_hbm, wqkv, 0)
    load_keys = local(pk_hbm.at[0], kall.at[pl.ds(0, cap)], 1)
    load_values = local(pv_hbm.at[0], vall.at[pl.ds(0, cap)], 2)
    load_out = local(wout_hbm, wout, 3)
    load_gu = local(wgu_hbm.at[c], wgu.at[own_rows], 4)
    load_down = local(wd_hbm.at[c], wd.at[own_rows], 5)

    barrier = pltpu.get_barrier_semaphore()

    def greet_group(k, carry):
        other = lax.rem(g + k, groups)
        pl.semaphore_signal(
            barrier, inc=1, device_id={"grp": other}, device_id_type=pl.DeviceIdType.MESH
        )
        return carry

    def greet_column(k, carry):
        other = lax.rem(e + k, columns)
        pl.semaphore_signal(
            barrier, inc=1, device_id={"exp": other}, device_id_type=pl.DeviceIdType.MESH
        )
        return carry

    lax.fori_loop(1, groups, greet_group, 0)
    lax.fori_loop(1, columns, greet_column, 0)

    for s in range(STEPS):
        xs[HALF * s : HALF * (s + 1), :] = x_ref[0, s].astype(F32)
        rts[HALF * s : HALF * (s + 1), :topk] = routes_ref[0, s]
    x16 = xs[...].astype(BF16)
    row_sub = iota((ROWS, HDIM), 0)
    row_lane = iota((ROWS, HDIM), 1)
    parent_hot = jnp.zeros((ROWS, HDIM), F32)
    for s in range(STEPS):
        for b in range(HALF):
            parent_hot = jnp.where(
                (row_sub == HALF * s + b) & (row_lane == par_ref[0, s, b]), 1.0, parent_hot
            )
    load_qkv.wait()
    qkv[0, :, 0 : 3 * HDIM] = dot(x16, wqkv[...]).astype(BF16)
    qkv[0, :, 3 * HDIM : 4 * HDIM] = parent_hot.astype(BF16)

    pl.semaphore_wait(barrier, groups + columns - 2)

    qkv_copy = remote(qkv.at[0], qkv.at[1], 0, grp=partner)
    qkv_copy.start()
    gain[pl.ds(c, 1)] = gain_in[...].reshape(1, 1, HDIM)
    wr[own_rows, :] = wr_in[...]
    swap_gain = remote(gain_in, gain.at[c], 1, exp=sibling)
    swap_router = remote(wr_in, wr.at[own_rows], 2, exp=sibling)
    swap_gu = remote(wgu_hbm.at[1 - c], wgu.at[own_rows], 3, exp=sibling)
    swap_down = remote(wd_hbm.at[1 - c], wd.at[own_rows], 4, exp=sibling)
    swap_gain.start()
    swap_router.start()
    swap_gu.start()
    swap_down.start()

    tail_at = cap
    new_at = cap + HALF * TAILP
    total = new_at + 2 * ROWS
    kall[tail_at:new_at, :] = jnp.zeros((HALF * TAILP, HDIM), BF16)
    vall[tail_at:new_at, :] = jnp.zeros((HALF * TAILP, HDIM), BF16)
    for b in range(HALF):
        at = tail_at + TAILP * b
        kall[at : at + PREV, :] = tk_ref[0, b]
        vall[at : at + PREV, :] = tv_ref[0, b]

    width = groups * SEND
    routes = rts[...]
    hit = jnp.zeros((ROWS, experts), jnp.bool_)
    expert_lane = iota((ROWS, experts), 1)
    for k in range(topk):
        hit = hit | (routes[:, k : k + 1] == expert_lane)
    hits = one_hot(hit)
    rank = dot(one_hot(iota((ROWS, ROWS), 1) < iota((ROWS, ROWS), 0)), hits)
    spread_row = iota((experts, width), 0)
    spread_lane = iota((experts, width), 1)
    spread = one_hot(spread_row == 2 * (spread_lane // SEND) + c)
    hit_wide = dot(hits, spread)
    rank_wide = dot(rank.astype(BF16), spread)
    slot_lane = (iota((ROWS, width), 1) % SEND).astype(F32)
    place = jnp.where((rank_wide == slot_lane) & (hit_wide > 0.5), 1.0, 0.0)

    load_keys.wait()
    load_values.wait()
    qkv_copy.wait_recv()
    for h in range(2):
        at = new_at + ROWS * h
        kall[at : at + ROWS, :] = qkv[h, :, HDIM : 2 * HDIM]
        vall[at : at + ROWS, :] = qkv[h, :, 2 * HDIM : 3 * HDIM]
    query = jnp.concatenate([qkv[0, :, 0:HDIM], qkv[1, :, 0:HDIM]], axis=0)
    parents = jnp.concatenate(
        [qkv[0, :, 3 * HDIM : 4 * HDIM], qkv[1, :, 3 * HDIM : 4 * HDIM]], axis=0
    )
    tokens = 2 * ROWS
    beam_row = iota((HDIM, tokens), 0)
    token_lane = iota((HDIM, tokens), 1)
    beam_of = HALF * ((token_lane // ROWS + half) % 2) + token_lane % HALF
    before = dot(parents, one_hot(beam_row == beam_of))
    step_row = (iota((tokens, tokens), 0) % ROWS) // HALF
    step_lane = (iota((tokens, tokens), 1) % ROWS) // HALF
    same = jnp.where(iota((tokens, tokens), 0) == iota((tokens, tokens), 1), 1.0, 0.0)
    back = jnp.where(step_lane + 1 == step_row, before, 0.0)
    back_bf = back.astype(BF16)
    near = (same + back).astype(BF16)
    back_two = dot(back_bf, back_bf)
    path = dot(near, (same + back_two).astype(BF16)).astype(BF16)
    first_row = iota((tokens, HDIM), 0) % ROWS
    first = jnp.where(first_row < HALF, parents.astype(F32), 0.0).astype(BF16)
    origin = dot(path, first).astype(BF16)
    tails = HALF * TAILP
    tail_row = iota((HDIM, tails), 0)
    tail_lane = iota((HDIM, tails), 1)
    tail_on = dot(
        origin,
        one_hot((tail_row == HALF * half + tail_lane // TAILP) & (tail_lane % TAILP < PREV)),
    )
    new_on = jnp.where(iota((tokens, tokens), 0) < ROWS, path.astype(F32), 0.0)

    score_scale = HDIM ** (-0.5)
    scores = dot_t(query, kall[...]) * score_scale
    prompt_live = iota((tokens, cap), 1) < parts_ref[0]
    prompt_s = jnp.where(prompt_live, scores[:, 0:cap], NEGATIVE)
    tail_s = jnp.where(tail_on > 0.5, scores[:, tail_at:new_at], NEGATIVE)
    new_s = jnp.where(new_on > 0.5, scores[:, new_at:total], NEGATIVE)
    top = jnp.maximum(
        jnp.maximum(
            jnp.max(prompt_s, axis=1, keepdims=True), jnp.max(tail_s, axis=1, keepdims=True)
        ),
        jnp.max(new_s, axis=1, keepdims=True),
    )
    prompt_w = jnp.exp(prompt_s - top)
    tail_w = jnp.exp(tail_s - top)
    new_w = jnp.exp(new_s - top)
    weight_sum = (
        jnp.sum(prompt_w, axis=1, keepdims=True)
        + jnp.sum(tail_w, axis=1, keepdims=True)
        + jnp.sum(new_w, axis=1, keepdims=True)
    )

    def weighted(weights, values):
        high, low = split_high(weights)
        both = dot(jnp.concatenate([high, low], axis=0), values)
        return both[0:tokens] + both[tokens : 2 * tokens]

    mix = (
        weighted(prompt_w, vall[0:cap, :])
        + weighted(tail_w, vall[tail_at:new_at, :])
        + weighted(new_w, vall[new_at:total, :])
    )
    part_send[:, 0:HDIM] = mix[ROWS:tokens]
    lane = iota((ROWS, HDIM), 1)
    part_send[:, HDIM : 2 * HDIM] = jnp.where(
        lane < HDIM // 2, top[ROWS:tokens], weight_sum[ROWS:tokens]
    )
    part_copy = remote(part_send, part_recv, 5, grp=partner)
    part_copy.start()
    load_out.wait()
    part_copy.wait_recv()
    far_mix = part_recv[:, 0:HDIM]
    far_top = part_recv[:, HDIM : HDIM + 1]
    far_sum = part_recv[:, HDIM + HDIM // 2 : HDIM + HDIM // 2 + 1]
    near_top = top[0:ROWS]
    best = jnp.maximum(near_top, far_top)
    near_factor = jnp.exp(near_top - best)
    far_factor = jnp.exp(far_top - best)
    attention = (
        (mix[0:ROWS] * near_factor + far_mix * far_factor)
        / (weight_sum[0:ROWS] * near_factor + far_sum * far_factor)
    ).astype(BF16)

    chip = 2 * HDIM
    proj = dot(attention, wout[...])
    for d in range(chips):
        proj_send[d] = proj[:, chip * d : chip * (d + 1)].astype(BF16)

    def send_proj(k, carry):
        other = lax.rem(e + k, columns)
        remote(proj_send.at[other // 2], proj_recv.at[e], 6, exp=other).start()
        return carry

    lax.fori_loop(1, columns, send_proj, 0)
    proj_recv[pl.ds(e, 1)] = proj_send[pl.ds(y, 1)]
    residual = xs[:, pl.ds(pl.multiple_of(y * chip, chip), chip)]
    wait_bytes(proj_recv.at[pl.ds(0, columns - 1)], recv_sem.at[6])
    residual = residual + jnp.sum(proj_recv[...].astype(F32), axis=0)

    rows_bf = residual.astype(BF16)
    outgoing = lax.dot_general(
        place.astype(BF16), rows_bf, (((0,), (0,)), ((), ())), preferred_element_type=F32
    ).astype(BF16)
    disp_send[...] = outgoing.reshape(groups, SEND, chip)

    def send_disp(k, carry):
        other = lax.rem(g + k, groups)
        remote(disp_send.at[other], disp_recv.at[g], 7, grp=other).start()
        return carry

    lax.fori_loop(1, groups, send_disp, 0)
    disp_recv[pl.ds(g, 1)] = disp_send[pl.ds(g, 1)]

    swap_gain.wait_recv()
    swap_router.wait_recv()
    gains = jnp.concatenate([gain[0], gain[1]], axis=1)
    logit_part = dot((residual * gains).astype(BF16), wr[...])
    stat_send[:, 0:experts] = logit_part
    stat_send[:, experts:HDIM] = jnp.broadcast_to(
        jnp.sum(residual * residual, axis=1, keepdims=True), (ROWS, HDIM - experts)
    )

    def send_stat(k, carry):
        other = lax.rem(y + k, chips)
        remote(stat_send, stat_recv.at[y], 8, exp=2 * other + c).start()
        return carry

    lax.fori_loop(1, chips, send_stat, 0)
    stat_recv[pl.ds(y, 1)] = stat_send[...].reshape(1, ROWS, stat_send.shape[1])

    wait_bytes(disp_recv.at[pl.ds(0, groups - 1)], recv_sem.at[7])
    arrived = disp_recv[...].reshape(groups * SEND, chip)
    packed = chips * PADB
    pick_row = iota((packed, groups * SEND), 0)
    pick_lane = iota((packed, groups * SEND), 1)
    per = BLOCK // CAP_E
    own_dest = pick_row // PADB

    def picks(shift):
        index = pick_row % PADB - shift
        safe = jnp.maximum(index, 0)
        source = (own_dest * per + safe // CAP_E) * SEND + safe % CAP_E
        return one_hot((index >= 0) & (index < BLOCK) & (pick_lane == source))

    gate_rows = dot(picks(0), arrived)
    up_rows = dot(picks(PADB - BLOCK), arrived)
    squares = dot_t(
        jnp.ones((8, chip), F32), gate_rows * gate_rows, precision=lax.Precision.HIGHEST
    )
    sq_send[...] = squares

    def send_sq(k, carry):
        other = lax.rem(y + k, chips)
        remote(sq_send, sq_recv.at[y], 9, exp=2 * other + c).start()
        return carry

    lax.fori_loop(1, chips, send_sq, 0)
    sq_recv[pl.ds(y, 1)] = squares.reshape(1, 8, packed)
    gate_in = (gate_rows * gains).astype(BF16)
    up_in = (up_rows * gains).astype(BF16)
    load_gu.wait()
    swap_gu.wait_recv()
    for t in range(ffe // HDIM):
        lanes = slice(HDIM * t, HDIM * (t + 1))
        gate = dot(gate_in, wgu[:, lanes]).reshape(chips, 2, 8, HDIM)
        up = dot(up_in, wgu[:, ffe + HDIM * t : ffe + HDIM * (t + 1)]).reshape(chips, 2, 8, HDIM)
        gu_send[:, 0:8, lanes] = gate[:, 0].astype(BF16)
        gu_send[:, 8:16, lanes] = (gate[:, 1] + up[:, 0]).astype(BF16)
        gu_send[:, 16:24, lanes] = up[:, 1].astype(BF16)

    def send_gu(k, carry):
        other = lax.rem(y + k, chips)
        remote(gu_send.at[other], gu_recv.at[y], 10, exp=2 * other + c).start()
        return carry

    lax.fori_loop(1, chips, send_gu, 0)
    gu_recv[pl.ds(y, 1)] = gu_send[pl.ds(y, 1)]

    wait_bytes(stat_recv.at[pl.ds(0, chips - 1)], recv_sem.at[8])
    stats = jnp.sum(stat_recv[...], axis=0)
    mean_square = stats[:, experts : experts + 1] / depth
    logits = stats[:, 0:experts] * lax.rsqrt(mean_square + EPSILON)
    picked_top = jnp.max(jnp.where(hit, logits, NEGATIVE), axis=1, keepdims=True)
    picked = jnp.where(hit, jnp.exp(jnp.minimum(logits - picked_top, 0.0)), 0.0)
    share = picked / jnp.sum(picked, axis=1, keepdims=True)
    share_high, share_low = split_high(share)
    shares = jnp.concatenate([share_high, share_low], axis=0)
    share_wide = dot(shares, spread)
    combine = jnp.concatenate(
        [
            (share_wide[0:ROWS] * place).astype(BF16),
            (share_wide[ROWS : 2 * ROWS] * place).astype(BF16),
        ],
        axis=0,
    )
    wait_bytes(sq_recv.at[pl.ds(0, chips - 1)], recv_sem.at[9])
    square_sums = jnp.sum(sq_recv[...], axis=0)[0:1, :]
    scale_row = iota((2 * BLOCK, packed), 0) % BLOCK
    scale_lane = iota((2 * BLOCK, packed), 1)
    own_square = jnp.sum(
        jnp.where(scale_lane == y * PADB + scale_row, square_sums, 0.0), axis=1, keepdims=True
    )
    scale = lax.rsqrt(own_square / depth + EPSILON)

    wait_bytes(gu_recv.at[pl.ds(0, chips - 1)], recv_sem.at[10])
    gsum[0 : 2 * BLOCK, :] = jnp.sum(gu_recv[...].astype(F32), axis=0) * scale
    gsum[2 * BLOCK : 2 * PADB, :] = jnp.zeros((2 * PADB - 2 * BLOCK, ffe), F32)
    gates = gsum[0:PADB, :]
    ups = gsum[BLOCK : BLOCK + PADB, :]
    hid[pl.ds(y, 1)] = (
        (gates / (1.0 + jnp.exp(-gates)) * ups).astype(BF16).reshape(1, PADB, ffe)
    )

    def send_hid(k, carry):
        other = lax.rem(y + k, chips)
        remote(hid.at[y], hid.at[y], 11, exp=2 * other + c).start()
        return carry

    lax.fori_loop(1, chips, send_hid, 0)
    load_down.wait()
    swap_down.wait_recv()
    back_row = iota((groups * SEND, packed), 0)
    back_lane = iota((groups * SEND, packed), 1)
    back_slot = back_row // SEND
    back_rank = back_row % SEND
    back_source = (back_slot // per) * PADB + (back_slot % per) * CAP_E + back_rank
    back_pick = one_hot((back_rank < CAP_E) & (back_lane == back_source))
    wait_bytes(hid.at[pl.ds(0, chips - 1)], recv_sem.at[11])
    result = dot_t(hid[...].reshape(packed, ffe), wd[...]).astype(BF16)
    ret_send[...] = dot(back_pick, result).astype(BF16).reshape(groups, SEND, chip)

    def send_ret(k, carry):
        other = lax.rem(g + k, groups)
        remote(ret_send.at[other], ret_recv.at[g], 12, grp=other).start()
        return carry

    lax.fori_loop(1, groups, send_ret, 0)
    ret_recv[pl.ds(g, 1)] = ret_send[pl.ds(g, 1)]
    wait_bytes(ret_recv.at[pl.ds(0, groups - 1)], recv_sem.at[12])
    both = dot(combine, ret_recv[...].reshape(groups * SEND, chip))
    expert_mix = both[0:ROWS] + both[ROWS : 2 * ROWS]
    mix_send[...] = jnp.where(c == 0, expert_mix[:, HDIM:chip], expert_mix[:, 0:HDIM])
    mix_copy = remote(mix_send, mix_recv, 13, exp=sibling)
    mix_copy.start()
    own = jnp.where(
        c == 0,
        residual[:, 0:HDIM] + expert_mix[:, 0:HDIM],
        residual[:, HDIM:chip] + expert_mix[:, HDIM:chip],
    )
    mix_copy.wait_recv()
    out_ref[...] = own + mix_recv[...]

    qkv_copy.wait_send()
    swap_gain.wait_send()
    swap_router.wait_send()
    swap_gu.wait_send()
    swap_down.wait_send()
    part_copy.wait_send()
    mix_copy.wait_send()
    wait_bytes(proj_recv.at[pl.ds(0, columns - 1)], send_sem.at[6])
    wait_bytes(disp_recv.at[pl.ds(0, groups - 1)], send_sem.at[7])
    wait_bytes(stat_recv.at[pl.ds(0, chips - 1)], send_sem.at[8])
    wait_bytes(sq_recv.at[pl.ds(0, chips - 1)], send_sem.at[9])
    wait_bytes(gu_recv.at[pl.ds(0, chips - 1)], send_sem.at[10])
    wait_bytes(hid.at[pl.ds(0, chips - 1)], send_sem.at[11])
    wait_bytes(ret_recv.at[pl.ds(0, groups - 1)], send_sem.at[12])


def on_device(
    step_inputs,
    parents,
    routes,
    w_qkv,
    w_out,
    prompt_keys,
    prompt_values,
    prompt_parts,
    tail_keys,
    tail_values,
    w_router,
    norm_gain,
    w_gate_up,
    w_down,
):
    groups = lax.axis_size("grp")
    columns = lax.axis_size("exp")
    chips = columns // 2
    depth = step_inputs.shape[3]
    cap = prompt_keys.shape[1]
    ffe = w_down.shape[2]
    experts = w_router.shape[1]
    topk = routes.shape[3]
    chip = 2 * HDIM
    keys = cap + HALF * TAILP + 2 * ROWS
    vmem = pl.BlockSpec(memory_space=pltpu.VMEM)
    smem = pl.BlockSpec(memory_space=pltpu.SMEM)
    anywhere = pl.BlockSpec(memory_space=pl.ANY)
    out = pl.pallas_call(
        functools.partial(kernel, groups, columns, topk),
        out_shape=jax.ShapeDtypeStruct((ROWS, HDIM), F32),
        in_specs=[
            vmem,
            smem,
            vmem,
            smem,
            vmem,
            vmem,
            anywhere,
            anywhere,
            anywhere,
            anywhere,
            vmem,
            vmem,
            anywhere,
            anywhere,
        ],
        out_specs=vmem,
        scratch_shapes=[
            pltpu.VMEM((ROWS, depth), F32),
            pltpu.VMEM((ROWS, HDIM), jnp.int32),
            pltpu.VMEM((2, 1, HDIM), F32),
            pltpu.VMEM((chip, experts), BF16),
            pltpu.VMEM((depth, 3 * HDIM), BF16),
            pltpu.VMEM((HDIM, depth), BF16),
            pltpu.VMEM((keys, HDIM), BF16),
            pltpu.VMEM((keys, HDIM), BF16),
            pltpu.VMEM((chip, 2 * ffe), BF16),
            pltpu.VMEM((chip, ffe), BF16),
            pltpu.VMEM((2, ROWS, 4 * HDIM), BF16),
            pltpu.VMEM((ROWS, chip), F32),
            pltpu.VMEM((ROWS, chip), F32),
            pltpu.VMEM((chips, ROWS, chip), BF16),
            pltpu.VMEM((columns, ROWS, chip), BF16),
            pltpu.VMEM((ROWS, HDIM), F32),
            pltpu.VMEM((chips, ROWS, HDIM), F32),
            pltpu.VMEM((groups, SEND, chip), BF16),
            pltpu.VMEM((groups, SEND, chip), BF16),
            pltpu.VMEM((8, chips * PADB), F32),
            pltpu.VMEM((chips, 8, chips * PADB), F32),
            pltpu.VMEM((chips, 2 * BLOCK, ffe), BF16),
            pltpu.VMEM((chips, 2 * BLOCK, ffe), BF16),
            pltpu.VMEM((2 * PADB, ffe), F32),
            pltpu.VMEM((chips, PADB, ffe), BF16),
            pltpu.VMEM((groups, SEND, chip), BF16),
            pltpu.VMEM((groups, SEND, chip), BF16),
            pltpu.VMEM((ROWS, HDIM), F32),
            pltpu.VMEM((ROWS, HDIM), F32),
            pltpu.SemaphoreType.DMA((6,)),
            pltpu.SemaphoreType.DMA((14,)),
            pltpu.SemaphoreType.DMA((14,)),
        ],
        compiler_params=pltpu.CompilerParams(
            collective_id=0, has_side_effects=True, vmem_limit_bytes=48 * 1024 * 1024
        ),
        name="layer",
    )(
        step_inputs,
        parents,
        routes,
        prompt_parts,
        norm_gain.reshape(1, HDIM),
        w_router,
        w_qkv.reshape(depth, 3 * HDIM),
        w_out,
        prompt_keys,
        prompt_values,
        tail_keys,
        tail_values,
        w_gate_up,
        w_down,
    )
    return out.astype(BF16).reshape(1, STEPS, HALF, HDIM)


def solution(mesh):
    placed = (
        P("grp", None, None, None),
        P("grp", None, None),
        P("grp", None, None, None),
        P(None, None, "exp"),
        P("exp", None),
        P("grp", None, "exp"),
        P("grp", None, "exp"),
        P("grp"),
        P("grp", None, None, "exp"),
        P("grp", None, None, "exp"),
        P("exp", None),
        P("exp"),
        P("grp", "exp", None),
        P("grp", "exp", None),
    )
    return jax.shard_map(
        on_device,
        mesh=mesh,
        in_specs=placed,
        out_specs=P("grp", None, None, "exp"),
        check_vma=False,
    )
```

time: 350 us -> 88 us (0.25)
  waiting for transfers between devices: 178 us -> 0 us
  blocking collectives: 86.7 us -> 0 us
  Pallas kernels: 0 us -> 70.8 us
  starting transfers between devices: 33.2 us -> 0 us
  between operations: 14.8 us -> 0.74 us
  other arithmetic: 10.9 us -> 0.6 us
  matrix products: 7.32 us -> 0 us
    psum x1 -> x0, waiting for transfers between devices: 112 us -> none  [on_device(): lax.psum(partial_units.astype(jnp.bfloat16), 'exp').astype(jnp.float32)]
    pallas_call x0 -> x1, Pallas kernels: none -> 70.8 us  [on_device(): pl.pallas_call(functools.partial(kernel, groups, columns, topk), out_shap...]
    reduce_scatter x1 -> x0, waiting for transfers between devices: 63.2 us -> none  [on_device(): lax.psum_scatter(proj_terms, 'exp', scatter_dimension=1, tiled=True)]
    psum x2 -> x0, blocking collectives: 50.5 us -> none  [the longest x1 25.3 us: on_device(): lax.psum(jnp.dot(normed, w_router, preferred_element_type=jnp.float32), '...]
    all_to_all x2 -> x0, blocking collectives: 36.2 us -> none  [the longest x1 18.6 us: on_device(): lax.all_to_all(expert_result.reshape(groups * local_experts * CAP_E, feat...]
    ppermute x12 -> x0, starting transfers between devices: 33.1 us -> none  [swapped(): return lax.ppermute(value, axis, pairs)]
    gather x16 -> x0, local copies, waits for them, and re-layouts: 9.88 us -> none  [the longest x4 3 us: on_device(): every_v[chosen].at[:, PREV + step_index]]
    unnamed x36 -> x28, local copies, waits for them, and re-layouts: 3.63 us -> 13.2 us
  transfers between devices with their start and end apart: 14 -> 0, of which waited for: 3 -> 0; matrix products, arithmetic and copies ran while one was open for 6% -> 0% of each run, Pallas kernels for 0% -> 0%
where the time goes in v1:
time: 88 us; the launch traced here: 87.4 us
  Pallas kernels  70.8 us (80%)
  local copies, waits for them, and re-layouts  15.3 us (17%)
    pallas_call x1, Pallas kernels, on_device(): pl.pallas_call(functools.partial(kernel, groups, columns, topk), out_shap...  70.8 us
    unnamed x28, local copies, waits for them, and re-layouts  13.2 us
    reshape x1, local copies, waits for them, and re-layouts, on_device(): w_qkv.reshape(depth, 3 * HDIM)  2.01 us

profile of v1, /device:TPU:1, one launch (start us, length us, event | category | flops | bytes accessed | tf_op | source)
XLA Modules:
  0.0 87.4 jit_solution(16072583238970661636)
XLA Ops:
  0.0 2.6 %copy.19 = bf16[2048,3,128]{0,2,1:T(8,128)(2,1)} copy(bf16[2048,3,128]{2,0,1:T(8,128)(2,1)} %param.17) | data formatting | bytes 3145728 | tf_op args[3]
  2.6 0.0 copy-start
  2.6 0.0 copy-start.2
  2.6 0.0 copy-start.9
  2.6 0.0 copy-start.10
  2.6 0.0 copy-start.11
  2.6 2.0 %copy.21.wqkv_hbm = bf16[2048,384]{1,0:T(8,128)(2,1)S(1)} copy(bf16[2048,384]{0,1:T(8,128)(2,1)} %bitcast.4) | data formatting | bytes 3145728 | tf_op jit(solution)/shard_map/reshape | solution.py:585
  4.6 1.5 %copy.22.tk_ref = bf16[1,4,60,128]{3,2,1,0:T(8,128)(2,1)} copy(bf16[1,4,60,128]{3,1,2,0:T(4,128)(2,1)} %param.22) | data formatting | bytes 122880 | tf_op args[8]
  6.1 1.5 %copy.23.tv_ref = bf16[1,4,60,128]{3,2,1,0:T(8,128)(2,1)} copy(bf16[1,4,60,128]{3,1,2,0:T(4,128)(2,1)} %param.23) | data formatting | bytes 122880 | tf_op args[9]
  7.6 1.4 %copy.20.wr_in = bf16[128,64]{1,0:T(8,128)(2,1)} copy(bf16[128,64]{0,1:T(8,128)(2,1)} %param.24) | data formatting | bytes 32768 | tf_op args[10]
  9.6 0.0 copy-done
  9.7 0.0 copy-done.2
  9.7 0.0 copy-done.9
  9.7 0.0 copy-done.10
  9.7 0.0 copy-done.11
  9.7 0.0 copy-start.1
  9.7 1.1 %copy-done.1 = bf16[2,128,1408]{2,1,0:T(8,128)(2,1)S(1)} copy-done((bf16[2,128,1408]{2,1,0:T(8,128)(2,1)S(1)}, bf16[2,128,1408]{2,1,0:T(8,128)(2,1)}, u32[]{:S(2)}) %copy-start.1) | copy-done | bytes 720920
  10.8 0.0 copy-start.3
  10.8 0.8 copy-done.3
  11.6 0.0 copy-start.4
  11.6 0.8 copy-done.4
  12.5 0.0 copy-start.5
  12.5 0.9 %copy-done.5 = bf16[1,1024,128]{2,1,0:T(8,128)(2,1)S(1)} copy-done((bf16[1,1024,128]{2,1,0:T(8,128)(2,1)S(1)}, bf16[1,1024,128]{2,1,0:T(8,128)(2,1)}, u32[]{:S(2)}) %copy-start.5) | copy-done | bytes 262168
  13.4 0.0 copy-start.6
  13.4 0.9 %copy-done.6 = bf16[1,1024,128]{2,1,0:T(8,128)(2,1)S(1)} copy-done((bf16[1,1024,128]{2,1,0:T(8,128)(2,1)S(1)}, bf16[1,1024,128]{2,1,0:T(8,128)(2,1)}, u32[]{:S(2)}) %copy-start.6) | copy-done | bytes 262168
  14.4 0.0 copy-start.7
  14.4 0.8 copy-done.7
  15.1 0.0 copy-start.8
  15.1 0.8 copy-done.8
  16.0 70.8 %layer.1 = f32[16,128]{1,0:T(8,128)S(1)} custom-call(bf16[1,4,4,2048]{3,2,1,0:T(4,128)(2,1)S(1)} %copy-done.8, s32[1,4,4]{2,1,0:T(4,128)S(1)} %copy-done.10, s32[1,4,4,6]{3,2,1,0:T(4,128)S(1)} %copy-done.9, s32[1]{0:T(128)S(6)} %copy.24.parts_ref, f32[1,128]{1,0:T(1,128)S(1)} %bitcast.3, bf16[128,64]{1,0:T(8,128)(2,1)S(1)} %copy-done.7, ...), custom_call_target="tpu_custom_call" | custom-call | tf_op jit(solution)/shard_map/layer/pallas_call | solution.py:520
  86.8 0.6 convert_element_type.3
Async XLA Ops:
  2.6 7.0 %copy-start = (bf16[2,128,2816]{2,1,0:T(8,128)(2,1)S(1)}, bf16[2,128,2816]{2,1,0:T(8,128)(2,1)}, u32[]{:S(2)}) copy-start(bf16[2,128,2816]{2,1,0:T(8,128)(2,1)} %wgu_hbm.1) | copy-start | bytes 4325380
  2.6 7.0 %copy-start.2 = (bf16[128,2048]{1,0:T(8,128)(2,1)S(1)}, bf16[128,2048]{1,0:T(8,128)(2,1)}, u32[]{:S(2)}) copy-start(bf16[128,2048]{1,0:T(8,128)(2,1)} %wout_hbm.1) | copy-start | bytes 1572868
  2.6 7.1 %copy-start.9 = (s32[1,4,4,6]{3,2,1,0:T(4,128)S(1)}, s32[1,4,4,6]{3,2,1,0:T(4,128)}, u32[]{:S(2)}) copy-start(s32[1,4,4,6]{3,2,1,0:T(4,128)} %routes_ref.1) | copy-start | bytes 1156
  2.6 7.1 %copy-start.10 = (s32[1,4,4]{2,1,0:T(4,128)S(1)}, s32[1,4,4]{2,1,0:T(4,128)}, u32[]{:S(2)}) copy-start(s32[1,4,4]{2,1,0:T(4,128)} %par_ref.1) | copy-start | bytes 196
  2.6 7.1 %copy-start.11 = (f32[128]{0:T(128)S(1)}, f32[128]{0:T(128)}, u32[]{:S(2)}) copy-start(f32[128]{0:T(128)} %param.25) | copy-start | bytes 1540
  9.7 1.1 %copy-start.1 = (bf16[2,128,1408]{2,1,0:T(8,128)(2,1)S(1)}, bf16[2,128,1408]{2,1,0:T(8,128)(2,1)}, u32[]{:S(2)}) copy-start(bf16[2,128,1408]{2,1,0:T(8,128)(2,1)} %wd_hbm.1) | copy-start | bytes 2162692
  10.8 0.8 copy-start.3
  11.6 0.8 copy-start.4
  12.5 0.9 %copy-start.5 = (bf16[1,1024,128]{2,1,0:T(8,128)(2,1)S(1)}, bf16[1,1024,128]{2,1,0:T(8,128)(2,1)}, u32[]{:S(2)}) copy-start(bf16[1,1024,128]{2,1,0:T(8,128)(2,1)} %pk_hbm.1) | copy-start | bytes 786436
  13.4 0.9 %copy-start.6 = (bf16[1,1024,128]{2,1,0:T(8,128)(2,1)S(1)}, bf16[1,1024,128]{2,1,0:T(8,128)(2,1)}, u32[]{:S(2)}) copy-start(bf16[1,1024,128]{2,1,0:T(8,128)(2,1)} %pv_hbm.1) | copy-start | bytes 786436
  14.4 0.8 copy-start.7
  15.1 0.8 copy-start.8

commit v2 on v1

--- a/solution.py
+++ b/solution.py
@@ -14,7 +14,6 @@
 ROWS = STEPS * HALF
 CAP_E = 3
 PREV = 60
-TAILP = 64
 SEND = 8
 BLOCK = 12
 PADB = 16
@@ -52,21 +51,27 @@
     groups,
     columns,
     topk,
+    x_hbm,
+    par_hbm,
+    routes_hbm,
+    parts_hbm,
+    gain_hbm,
+    wr_hbm,
+    wqkv_hbm,
+    wout_hbm,
+    pk_hbm,
+    pv_hbm,
+    tk_hbm,
+    tv_hbm,
+    wgu_hbm,
+    wd_hbm,
+    out_ref,
     x_ref,
     par_ref,
     routes_ref,
     parts_ref,
-    gain_in,
-    wr_in,
-    wqkv_hbm,
-    wout_hbm,
-    pk_hbm,
-    pv_hbm,
     tk_ref,
     tv_ref,
-    wgu_hbm,
-    wd_hbm,
-    out_ref,
     xs,
     rts,
     gain,
@@ -104,7 +109,7 @@
     ffe = wd.shape[1]
     cap = pk_hbm.shape[1]
     experts = wr.shape[1]
-    depth = x_ref.shape[3]
+    depth = x_ref.shape[2]
     g = lax.axis_index("grp")
     e = lax.axis_index("exp")
     y = e // 2
@@ -132,7 +137,15 @@
     def wait_bytes(ref, sem):
         pltpu.make_async_copy(ref, ref, sem).wait()
 
+    load_inputs = local(x_hbm.at[0], x_ref, 6)
+    load_parents = local(par_hbm, par_ref, 7)
+    load_routes = local(routes_hbm.at[0], routes_ref, 8)
+    load_parts = local(parts_hbm, parts_ref, 9)
     load_qkv = local(wqkv_hbm, wqkv, 0)
+    load_tail_k = local(tk_hbm.at[0], tk_ref, 10)
+    load_tail_v = local(tv_hbm.at[0], tv_ref, 11)
+    load_gain = local(gain_hbm, gain.at[c], 12)
+    load_router = local(wr_hbm, wr.at[c], 13)
     load_keys = local(pk_hbm.at[0], kall.at[pl.ds(0, cap)], 1)
     load_values = local(pv_hbm.at[0], vall.at[pl.ds(0, cap)], 2)
     load_out = local(wout_hbm, wout, 3)
@@ -158,9 +171,12 @@
     lax.fori_loop(1, groups, greet_group, 0)
     lax.fori_loop(1, columns, greet_column, 0)
 
+    load_inputs.wait()
+    load_routes.wait()
+    load_parents.wait()
     for s in range(STEPS):
-        xs[HALF * s : HALF * (s + 1), :] = x_ref[0, s].astype(F32)
-        rts[HALF * s : HALF * (s + 1), :topk] = routes_ref[0, s]
+        xs[HALF * s : HALF * (s + 1), :] = x_ref[s].astype(F32)
+        rts[HALF * s : HALF * (s + 1), :topk] = routes_ref[s]
     x16 = xs[...].astype(BF16)
     row_sub = iota((ROWS, HDIM), 0)
     row_lane = iota((ROWS, HDIM), 1)
@@ -171,17 +187,16 @@
                 (row_sub == HALF * s + b) & (row_lane == par_ref[0, s, b]), 1.0, parent_hot
             )
     load_qkv.wait()
-    qkv[0, :, 0 : 3 * HDIM] = dot(x16, wqkv[...]).astype(BF16)
+    for i in range(3):
+        qkv[0, :, HDIM * i : HDIM * (i + 1)] = dot(x16, wqkv[i]).astype(BF16)
     qkv[0, :, 3 * HDIM : 4 * HDIM] = parent_hot.astype(BF16)
 
     pl.semaphore_wait(barrier, groups + columns - 2)
 
     qkv_copy = remote(qkv.at[0], qkv.at[1], 0, grp=partner)
     qkv_copy.start()
-    gain[pl.ds(c, 1)] = gain_in[...].reshape(1, 1, HDIM)
-    wr[own_rows, :] = wr_in[...]
-    swap_gain = remote(gain_in, gain.at[c], 1, exp=sibling)
-    swap_router = remote(wr_in, wr.at[own_rows], 2, exp=sibling)
+    swap_gain = remote(gain_hbm, gain.at[c], 1, exp=sibling)
+    swap_router = remote(wr_hbm, wr.at[c], 2, exp=sibling)
     swap_gu = remote(wgu_hbm.at[1 - c], wgu.at[own_rows], 3, exp=sibling)
     swap_down = remote(wd_hbm.at[1 - c], wd.at[own_rows], 4, exp=sibling)
     swap_gain.start()
@@ -190,14 +205,12 @@
     swap_down.start()
 
     tail_at = cap
-    new_at = cap + HALF * TAILP
+    new_at = cap + HALF * PREV
     total = new_at + 2 * ROWS
-    kall[tail_at:new_at, :] = jnp.zeros((HALF * TAILP, HDIM), BF16)
-    vall[tail_at:new_at, :] = jnp.zeros((HALF * TAILP, HDIM), BF16)
-    for b in range(HALF):
-        at = tail_at + TAILP * b
-        kall[at : at + PREV, :] = tk_ref[0, b]
-        vall[at : at + PREV, :] = tv_ref[0, b]
+    load_tail_k.wait()
+    load_tail_v.wait()
+    kall[tail_at:new_at, :] = tk_ref[...].astype(F32).reshape(HALF * PREV, HDIM).astype(BF16)
+    vall[tail_at:new_at, :] = tv_ref[...].astype(F32).reshape(HALF * PREV, HDIM).astype(BF16)
 
     width = groups * SEND
     routes = rts[...]
@@ -242,15 +255,13 @@
     first_row = iota((tokens, HDIM), 0) % ROWS
     first = jnp.where(first_row < HALF, parents.astype(F32), 0.0).astype(BF16)
     origin = dot(path, first).astype(BF16)
-    tails = HALF * TAILP
+    tails = HALF * PREV
     tail_row = iota((HDIM, tails), 0)
     tail_lane = iota((HDIM, tails), 1)
-    tail_on = dot(
-        origin,
-        one_hot((tail_row == HALF * half + tail_lane // TAILP) & (tail_lane % TAILP < PREV)),
-    )
+    tail_on = dot(origin, one_hot(tail_row == HALF * half + tail_lane % HALF))
     new_on = jnp.where(iota((tokens, tokens), 0) < ROWS, path.astype(F32), 0.0)
 
+    load_parts.wait()
     score_scale = HDIM ** (-0.5)
     scores = dot_t(query, kall[...]) * score_scale
     prompt_live = iota((tokens, cap), 1) < parts_ref[0]
@@ -333,10 +344,13 @@
     lax.fori_loop(1, groups, send_disp, 0)
     disp_recv[pl.ds(g, 1)] = disp_send[pl.ds(g, 1)]
 
+    load_gain.wait()
+    load_router.wait()
     swap_gain.wait_recv()
     swap_router.wait_recv()
     gains = jnp.concatenate([gain[0], gain[1]], axis=1)
-    logit_part = dot((residual * gains).astype(BF16), wr[...])
+    scaled = (residual * gains).astype(BF16)
+    logit_part = dot_t(scaled[:, 0:HDIM], wr[0]) + dot_t(scaled[:, HDIM:chip], wr[1])
     stat_send[:, 0:experts] = logit_part
     stat_send[:, experts:HDIM] = jnp.broadcast_to(
         jnp.sum(residual * residual, axis=1, keepdims=True), (ROWS, HDIM - experts)
@@ -513,36 +527,28 @@
     experts = w_router.shape[1]
     topk = routes.shape[3]
     chip = 2 * HDIM
-    keys = cap + HALF * TAILP + 2 * ROWS
+    keys = cap + HALF * PREV + 2 * ROWS
     vmem = pl.BlockSpec(memory_space=pltpu.VMEM)
-    smem = pl.BlockSpec(memory_space=pltpu.SMEM)
-    anywhere = pl.BlockSpec(memory_space=pl.ANY)
     out = pl.pallas_call(
         functools.partial(kernel, groups, columns, topk),
         out_shape=jax.ShapeDtypeStruct((ROWS, HDIM), F32),
         in_specs=[
-            vmem,
-            smem,
-            vmem,
-            smem,
-            vmem,
-            vmem,
-            anywhere,
-            anywhere,
-            anywhere,
-            anywhere,
-            vmem,
-            vmem,
-            anywhere,
-            anywhere,
-        ],
+            pl.BlockSpec(memory_space=pltpu.HBM)
+        ]
+        * 14,
         out_specs=vmem,
         scratch_shapes=[
+            pltpu.VMEM((STEPS, HALF, depth), BF16),
+            pltpu.SMEM((1, STEPS, HALF), jnp.int32),
+            pltpu.VMEM((STEPS, HALF, topk), jnp.int32),
+            pltpu.SMEM((1,), jnp.int32),
+            pltpu.VMEM((PREV, HALF, HDIM), BF16),
+            pltpu.VMEM((PREV, HALF, HDIM), BF16),
             pltpu.VMEM((ROWS, depth), F32),
             pltpu.VMEM((ROWS, HDIM), jnp.int32),
             pltpu.VMEM((2, 1, HDIM), F32),
-            pltpu.VMEM((chip, experts), BF16),
-            pltpu.VMEM((depth, 3 * HDIM), BF16),
+            pltpu.VMEM((2, experts, HDIM), BF16),
+            pltpu.VMEM((3, depth, HDIM), BF16),
             pltpu.VMEM((HDIM, depth), BF16),
             pltpu.VMEM((keys, HDIM), BF16),
             pltpu.VMEM((keys, HDIM), BF16),
@@ -567,12 +573,12 @@
             pltpu.VMEM((groups, SEND, chip), BF16),
             pltpu.VMEM((ROWS, HDIM), F32),
             pltpu.VMEM((ROWS, HDIM), F32),
-            pltpu.SemaphoreType.DMA((6,)),
+            pltpu.SemaphoreType.DMA((14,)),
             pltpu.SemaphoreType.DMA((14,)),
             pltpu.SemaphoreType.DMA((14,)),
         ],
         compiler_params=pltpu.CompilerParams(
-            collective_id=0, has_side_effects=True, vmem_limit_bytes=48 * 1024 * 1024
+            collective_id=0, has_side_effects=True, vmem_limit_bytes=64 * 1024 * 1024
         ),
         name="layer",
     )(
@@ -581,13 +587,13 @@
         routes,
         prompt_parts,
         norm_gain.reshape(1, HDIM),
-        w_router,
-        w_qkv.reshape(depth, 3 * HDIM),
+        w_router.T,
+        jnp.transpose(w_qkv, (1, 0, 2)),
         w_out,
         prompt_keys,
         prompt_values,
-        tail_keys,
-        tail_values,
+        jnp.transpose(tail_keys, (0, 2, 1, 3)),
+        jnp.transpose(tail_values, (0, 2, 1, 3)),
         w_gate_up,
         w_down,
     )

time: 88 us -> 72.8 us (0.83)
  local copies, waits for them, and re-layouts: 15.3 us -> 0 us
    unnamed x28 -> x0, local copies, waits for them, and re-layouts: 13.2 us -> none
    reshape x1 -> x0, local copies, waits for them, and re-layouts: 2.01 us -> none  [on_device(): w_qkv.reshape(depth, 3 * HDIM)]
where the time goes in v2:
time: 72.8 us; the launch traced here: 72.6 us
  Pallas kernels  70.7 us (97%)
  other arithmetic  1.29 us (2%)
    pallas_call x1, Pallas kernels, on_device(): pl.pallas_call(functools.partial(kernel, groups, columns, topk), out_shap...  70.7 us

profile of v2, /device:TPU:1, one launch (start us, length us, event | category | flops | bytes accessed | tf_op | source)
XLA Modules:
  0.0 72.6 jit_solution(13051349965572042840)
XLA Ops:
  0.7 70.7 %layer.1 = f32[16,128]{1,0:T(8,128)} custom-call(bf16[1,4,4,2048]{3,2,1,0:T(4,128)(2,1)} %x_hbm.1, s32[1,4,4]{2,1,0:T(4,128)} %par_hbm.1, s32[1,4,4,6]{3,2,1,0:T(4,128)} %routes_hbm.1, s32[1]{0:T(128)S(6)} %copy.15.parts_hbm, f32[1,128]{1,0:T(1,128)} %bitcast.10, bf16[64,128]{1,0:T(8,128)(2,1)} %bitcast.9, bf16[3,2048,128]{2,1,0:T(8,128)(2,1)} %bitcast.6, ...), custom_call_target="tpu_custom_call" | custom-call | tf_op jit(solution)/shard_map/layer/pallas_call | solution.py:532
  71.3 1.3 %convert_element_type.3 = bf16[16,128]{1,0:T(8,128)(2,1)} convert(f32[16,128]{1,0:T(8,128)} %layer.1) | non-fusion elementwise | flops 2048 | bytes 12288 | tf_op jit(solution)/shard_map/convert_element_type | solution.py:600

commit v3 on v2

--- a/solution.py
+++ b/solution.py
@@ -14,7 +14,7 @@
 ROWS = STEPS * HALF
 CAP_E = 3
 PREV = 60
-SEND = 8
+SEND = 4
 BLOCK = 12
 PADB = 16
 
@@ -45,6 +45,11 @@
 def split_high(value):
     high = value.astype(BF16)
     return high, (value - high.astype(F32)).astype(BF16)
+
+
+def column_spans(ffe):
+    first = (ffe // HDIM + 1) // 2 * HDIM
+    return (0, first), (first, ffe - first)
 
 
 def kernel(
@@ -85,6 +90,7 @@
     qkv,
     part_send,
     part_recv,
+    att,
     proj_send,
     proj_recv,
     stat_send,
@@ -94,6 +100,8 @@
     sq_send,
     sq_recv,
     gu_send,
+    gu_mid,
+    gu_pass,
     gu_recv,
     gsum,
     hid,
@@ -107,6 +115,7 @@
 ):
     chips = columns // 2
     ffe = wd.shape[1]
+    spans = column_spans(ffe)
     cap = pk_hbm.shape[1]
     experts = wr.shape[1]
     depth = x_ref.shape[2]
@@ -119,10 +128,19 @@
     sibling = e + 1 - 2 * c
     own_rows = pl.ds(pl.multiple_of(c * HDIM, HDIM), HDIM)
 
+    waits = {}
+
+    def done(kind, index):
+        waits.pop((kind, index))()
+
+    def finish():
+        for key in list(waits):
+            done(*key)
+
     def local(src, dst, index):
         copy = pltpu.make_async_copy(src, dst, local_sem.at[index])
         copy.start()
-        return copy
+        waits["load", index] = copy.wait
 
     def remote(src, dst, index, **where):
         return pltpu.make_async_remote_copy(
@@ -134,23 +152,45 @@
             device_id_type=pl.DeviceIdType.MESH,
         )
 
-    def wait_bytes(ref, sem):
-        pltpu.make_async_copy(ref, ref, sem).wait()
-
-    load_inputs = local(x_hbm.at[0], x_ref, 6)
-    load_parents = local(par_hbm, par_ref, 7)
-    load_routes = local(routes_hbm.at[0], routes_ref, 8)
-    load_parts = local(parts_hbm, parts_ref, 9)
-    load_qkv = local(wqkv_hbm, wqkv, 0)
-    load_tail_k = local(tk_hbm.at[0], tk_ref, 10)
-    load_tail_v = local(tv_hbm.at[0], tv_ref, 11)
-    load_gain = local(gain_hbm, gain.at[c], 12)
-    load_router = local(wr_hbm, wr.at[c], 13)
-    load_keys = local(pk_hbm.at[0], kall.at[pl.ds(0, cap)], 1)
-    load_values = local(pv_hbm.at[0], vall.at[pl.ds(0, cap)], 2)
-    load_out = local(wout_hbm, wout, 3)
-    load_gu = local(wgu_hbm.at[c], wgu.at[own_rows], 4)
-    load_down = local(wd_hbm.at[c], wd.at[own_rows], 5)
+    def send(src, dst, index, **where):
+        copy = remote(src, dst, index, **where)
+        copy.start()
+        waits["recv", index] = copy.wait_recv
+        waits["send", index] = copy.wait_send
+
+    def send_each(count, one, landing, index):
+        def step(k, carry):
+            one(k).start()
+            return carry
+
+        lax.fori_loop(1, count, step, 0)
+        whole = landing.at[pl.ds(0, count - 1)]
+        waits["recv", index] = pltpu.make_async_copy(whole, whole, recv_sem.at[index]).wait
+        waits["send", index] = pltpu.make_async_copy(whole, whole, send_sem.at[index]).wait
+
+    def other_group(k):
+        return lax.rem(g + k, groups)
+
+    def other_column(k):
+        return lax.rem(e + k, columns)
+
+    def other_chip(k):
+        return lax.rem(y + k, chips)
+
+    local(x_hbm.at[0], x_ref, 6)
+    local(par_hbm, par_ref, 7)
+    local(routes_hbm.at[0], routes_ref, 8)
+    local(parts_hbm, parts_ref, 9)
+    local(wqkv_hbm, wqkv, 0)
+    local(tk_hbm.at[0], tk_ref, 10)
+    local(tv_hbm.at[0], tv_ref, 11)
+    local(gain_hbm, gain.at[c], 12)
+    local(wr_hbm, wr.at[c], 13)
+    local(pk_hbm.at[0], kall.at[pl.ds(0, cap)], 1)
+    local(pv_hbm.at[0], vall.at[pl.ds(0, cap)], 2)
+    local(wout_hbm, wout.at[own_rows], 3)
+    local(wgu_hbm.at[c], wgu.at[own_rows], 4)
+    local(wd_hbm.at[c], wd.at[own_rows], 5)
 
     barrier = pltpu.get_barrier_semaphore()
 
@@ -171,9 +211,9 @@
     lax.fori_loop(1, groups, greet_group, 0)
     lax.fori_loop(1, columns, greet_column, 0)
 
-    load_inputs.wait()
-    load_routes.wait()
-    load_parents.wait()
+    done("load", 6)
+    done("load", 8)
+    done("load", 7)
     for s in range(STEPS):
         xs[HALF * s : HALF * (s + 1), :] = x_ref[s].astype(F32)
         rts[HALF * s : HALF * (s + 1), :topk] = routes_ref[s]
@@ -186,29 +226,25 @@
             parent_hot = jnp.where(
                 (row_sub == HALF * s + b) & (row_lane == par_ref[0, s, b]), 1.0, parent_hot
             )
-    load_qkv.wait()
+    done("load", 0)
     for i in range(3):
         qkv[0, :, HDIM * i : HDIM * (i + 1)] = dot(x16, wqkv[i]).astype(BF16)
     qkv[0, :, 3 * HDIM : 4 * HDIM] = parent_hot.astype(BF16)
 
     pl.semaphore_wait(barrier, groups + columns - 2)
 
-    qkv_copy = remote(qkv.at[0], qkv.at[1], 0, grp=partner)
-    qkv_copy.start()
-    swap_gain = remote(gain_hbm, gain.at[c], 1, exp=sibling)
-    swap_router = remote(wr_hbm, wr.at[c], 2, exp=sibling)
-    swap_gu = remote(wgu_hbm.at[1 - c], wgu.at[own_rows], 3, exp=sibling)
-    swap_down = remote(wd_hbm.at[1 - c], wd.at[own_rows], 4, exp=sibling)
-    swap_gain.start()
-    swap_router.start()
-    swap_gu.start()
-    swap_down.start()
+    send(qkv.at[0], qkv.at[1], 0, grp=partner)
+    send(wout_hbm, wout.at[own_rows], 6, exp=sibling)
+    send(gain_hbm, gain.at[c], 1, exp=sibling)
+    send(wr_hbm, wr.at[c], 2, exp=sibling)
+    send(wgu_hbm.at[1 - c], wgu.at[own_rows], 3, exp=sibling)
+    send(wd_hbm.at[1 - c], wd.at[own_rows], 4, exp=sibling)
 
     tail_at = cap
     new_at = cap + HALF * PREV
     total = new_at + 2 * ROWS
-    load_tail_k.wait()
-    load_tail_v.wait()
+    done("load", 10)
+    done("load", 11)
     kall[tail_at:new_at, :] = tk_ref[...].astype(F32).reshape(HALF * PREV, HDIM).astype(BF16)
     vall[tail_at:new_at, :] = tv_ref[...].astype(F32).reshape(HALF * PREV, HDIM).astype(BF16)
 
@@ -228,9 +264,9 @@
     slot_lane = (iota((ROWS, width), 1) % SEND).astype(F32)
     place = jnp.where((rank_wide == slot_lane) & (hit_wide > 0.5), 1.0, 0.0)
 
-    load_keys.wait()
-    load_values.wait()
-    qkv_copy.wait_recv()
+    done("load", 1)
+    done("load", 2)
+    done("recv", 0)
     for h in range(2):
         at = new_at + ROWS * h
         kall[at : at + ROWS, :] = qkv[h, :, HDIM : 2 * HDIM]
@@ -261,7 +297,7 @@
     tail_on = dot(origin, one_hot(tail_row == HALF * half + tail_lane % HALF))
     new_on = jnp.where(iota((tokens, tokens), 0) < ROWS, path.astype(F32), 0.0)
 
-    load_parts.wait()
+    done("load", 9)
     score_scale = HDIM ** (-0.5)
     scores = dot_t(query, kall[...]) * score_scale
     prompt_live = iota((tokens, cap), 1) < parts_ref[0]
@@ -298,10 +334,8 @@
     part_send[:, HDIM : 2 * HDIM] = jnp.where(
         lane < HDIM // 2, top[ROWS:tokens], weight_sum[ROWS:tokens]
     )
-    part_copy = remote(part_send, part_recv, 5, grp=partner)
-    part_copy.start()
-    load_out.wait()
-    part_copy.wait_recv()
+    send(part_send, part_recv, 5, grp=partner)
+    done("recv", 5)
     far_mix = part_recv[:, 0:HDIM]
     far_top = part_recv[:, HDIM : HDIM + 1]
     far_sum = part_recv[:, HDIM + HDIM // 2 : HDIM + HDIM // 2 + 1]
@@ -309,45 +343,52 @@
     best = jnp.maximum(near_top, far_top)
     near_factor = jnp.exp(near_top - best)
     far_factor = jnp.exp(far_top - best)
-    attention = (
+    att[pl.ds(c, 1)] = (
         (mix[0:ROWS] * near_factor + far_mix * far_factor)
         / (weight_sum[0:ROWS] * near_factor + far_sum * far_factor)
-    ).astype(BF16)
+    ).astype(BF16).reshape(1, ROWS, HDIM)
+    send(att.at[c], att.at[c], 14, exp=sibling)
+    done("load", 3)
+    done("recv", 6)
+    done("recv", 14)
 
     chip = 2 * HDIM
-    proj = dot(attention, wout[...])
+    proj = dot(jnp.concatenate([att[0], att[1]], axis=1), wout[...])
     for d in range(chips):
         proj_send[d] = proj[:, chip * d : chip * (d + 1)].astype(BF16)
-
-    def send_proj(k, carry):
-        other = lax.rem(e + k, columns)
-        remote(proj_send.at[other // 2], proj_recv.at[e], 6, exp=other).start()
-        return carry
-
-    lax.fori_loop(1, columns, send_proj, 0)
-    proj_recv[pl.ds(e, 1)] = proj_send[pl.ds(y, 1)]
+    send_each(
+        chips,
+        lambda k: remote(
+            proj_send.at[other_chip(k)], proj_recv.at[y], 15, exp=2 * other_chip(k) + c
+        ),
+        proj_recv,
+        15,
+    )
+    proj_recv[pl.ds(y, 1)] = proj_send[pl.ds(y, 1)]
     residual = xs[:, pl.ds(pl.multiple_of(y * chip, chip), chip)]
-    wait_bytes(proj_recv.at[pl.ds(0, columns - 1)], recv_sem.at[6])
+    done("recv", 15)
     residual = residual + jnp.sum(proj_recv[...].astype(F32), axis=0)
 
     rows_bf = residual.astype(BF16)
     outgoing = lax.dot_general(
         place.astype(BF16), rows_bf, (((0,), (0,)), ((), ())), preferred_element_type=F32
-    ).astype(BF16)
-    disp_send[...] = outgoing.reshape(groups, SEND, chip)
-
-    def send_disp(k, carry):
-        other = lax.rem(g + k, groups)
-        remote(disp_send.at[other], disp_recv.at[g], 7, grp=other).start()
-        return carry
-
-    lax.fori_loop(1, groups, send_disp, 0)
+    )
+    disp_send[...] = outgoing.reshape(groups, SEND, chip).astype(BF16)
+
+    send_each(
+        groups,
+        lambda k: remote(
+            disp_send.at[other_group(k)], disp_recv.at[g], 7, grp=other_group(k)
+        ),
+        disp_recv,
+        7,
+    )
     disp_recv[pl.ds(g, 1)] = disp_send[pl.ds(g, 1)]
 
-    load_gain.wait()
-    load_router.wait()
-    swap_gain.wait_recv()
-    swap_router.wait_recv()
+    done("load", 12)
+    done("load", 13)
+    done("recv", 1)
+    done("recv", 2)
     gains = jnp.concatenate([gain[0], gain[1]], axis=1)
     scaled = (residual * gains).astype(BF16)
     logit_part = dot_t(scaled[:, 0:HDIM], wr[0]) + dot_t(scaled[:, HDIM:chip], wr[1])
@@ -356,16 +397,14 @@
         jnp.sum(residual * residual, axis=1, keepdims=True), (ROWS, HDIM - experts)
     )
 
-    def send_stat(k, carry):
-        other = lax.rem(y + k, chips)
-        remote(stat_send, stat_recv.at[y], 8, exp=2 * other + c).start()
-        return carry
-
-    lax.fori_loop(1, chips, send_stat, 0)
+    send_each(
+        chips,
+        lambda k: remote(stat_send, stat_recv.at[y], 8, exp=2 * other_chip(k) + c),
+        stat_recv,
+        8,
+    )
     stat_recv[pl.ds(y, 1)] = stat_send[...].reshape(1, ROWS, stat_send.shape[1])
 
-    wait_bytes(disp_recv.at[pl.ds(0, groups - 1)], recv_sem.at[7])
-    arrived = disp_recv[...].reshape(groups * SEND, chip)
     packed = chips * PADB
     pick_row = iota((packed, groups * SEND), 0)
     pick_lane = iota((packed, groups * SEND), 1)
@@ -378,41 +417,66 @@
         source = (own_dest * per + safe // CAP_E) * SEND + safe % CAP_E
         return one_hot((index >= 0) & (index < BLOCK) & (pick_lane == source))
 
-    gate_rows = dot(picks(0), arrived)
-    up_rows = dot(picks(PADB - BLOCK), arrived)
+    gate_pick = picks(0)
+    up_pick = picks(PADB - BLOCK)
+    done("recv", 7)
+    arrived = disp_recv[...].astype(F32).reshape(groups * SEND, chip).astype(BF16)
+    gate_rows = dot(gate_pick, arrived)
+    up_rows = dot(up_pick, arrived)
     squares = dot_t(
         jnp.ones((8, chip), F32), gate_rows * gate_rows, precision=lax.Precision.HIGHEST
     )
     sq_send[...] = squares
 
-    def send_sq(k, carry):
-        other = lax.rem(y + k, chips)
-        remote(sq_send, sq_recv.at[y], 9, exp=2 * other + c).start()
-        return carry
-
-    lax.fori_loop(1, chips, send_sq, 0)
+    send_each(
+        chips,
+        lambda k: remote(sq_send, sq_recv.at[y], 9, exp=2 * other_chip(k) + c),
+        sq_recv,
+        9,
+    )
     sq_recv[pl.ds(y, 1)] = squares.reshape(1, 8, packed)
     gate_in = (gate_rows * gains).astype(BF16)
     up_in = (up_rows * gains).astype(BF16)
-    load_gu.wait()
-    swap_gu.wait_recv()
-    for t in range(ffe // HDIM):
-        lanes = slice(HDIM * t, HDIM * (t + 1))
-        gate = dot(gate_in, wgu[:, lanes]).reshape(chips, 2, 8, HDIM)
-        up = dot(up_in, wgu[:, ffe + HDIM * t : ffe + HDIM * (t + 1)]).reshape(chips, 2, 8, HDIM)
-        gu_send[:, 0:8, lanes] = gate[:, 0].astype(BF16)
-        gu_send[:, 8:16, lanes] = (gate[:, 1] + up[:, 0]).astype(BF16)
-        gu_send[:, 16:24, lanes] = up[:, 1].astype(BF16)
-
-    def send_gu(k, carry):
-        other = lax.rem(y + k, chips)
-        remote(gu_send.at[other], gu_recv.at[y], 10, exp=2 * other + c).start()
-        return carry
-
-    lax.fori_loop(1, chips, send_gu, 0)
-    gu_recv[pl.ds(y, 1)] = gu_send[pl.ds(y, 1)]
-
-    wait_bytes(stat_recv.at[pl.ds(0, chips - 1)], recv_sem.at[8])
+    done("load", 4)
+    done("recv", 3)
+    def to_chip(src, dst, index, offset):
+        send(src, dst, index, exp=2 * lax.rem(y + offset + chips, chips) + c)
+
+    def rows_of(offset):
+        return lax.rem(y + offset + chips, chips)
+
+    for h in range(2):
+        first, size = spans[h]
+        for at in range(first, first + size, chip):
+            wide = min(chip, first + size - at)
+            gate = dot(gate_in, wgu[:, at : at + wide]).reshape(chips, 2, 8, wide)
+            up = dot(up_in, wgu[:, ffe + at : ffe + at + wide]).reshape(chips, 2, 8, wide)
+            lanes = slice(at - first, at - first + wide)
+            gu_send[h][:, 0:8, lanes] = gate[:, 0].astype(BF16)
+            gu_send[h][:, 8:16, lanes] = (gate[:, 1] + up[:, 0]).astype(BF16)
+            gu_send[h][:, 16:24, lanes] = up[:, 1].astype(BF16)
+        base = 16 + 7 * h
+        far = 1 - 2 * h
+        to_chip(gu_send[h].at[rows_of(4)], gu_mid[h].at[2], base + 2, 2 * far)
+        to_chip(gu_send[h].at[rows_of(3)], gu_mid[h].at[0], base, 1)
+        to_chip(gu_send[h].at[rows_of(-3)], gu_mid[h].at[1], base + 1, -1)
+        to_chip(gu_send[h].at[rows_of(1)], gu_recv[h].at[0], base + 3, 1)
+        to_chip(gu_send[h].at[rows_of(-1)], gu_recv[h].at[1], base + 4, -1)
+    for h in range(2):
+        base = 16 + 7 * h
+        done("recv", base)
+        done("recv", base + 1)
+        done("recv", base + 2)
+        for i in range(2):
+            direction = 1 - 2 * i
+            passing = gu_send[h][pl.ds(rows_of(2 * direction), 1)][0].astype(F32)
+            passing = passing + gu_mid[h][i].astype(F32)
+            if i == h:
+                passing = passing + gu_mid[h][2].astype(F32)
+            gu_pass[h][i] = passing.astype(BF16)
+            to_chip(gu_pass[h].at[i], gu_recv[h].at[2 + i], base + 5 + i, 2 * direction)
+
+    done("recv", 8)
     stats = jnp.sum(stat_recv[...], axis=0)
     mean_square = stats[:, experts : experts + 1] / depth
     logits = stats[:, 0:experts] * lax.rsqrt(mean_square + EPSILON)
@@ -429,7 +493,7 @@
         ],
         axis=0,
     )
-    wait_bytes(sq_recv.at[pl.ds(0, chips - 1)], recv_sem.at[9])
+    done("recv", 9)
     square_sums = jnp.sum(sq_recv[...], axis=0)[0:1, :]
     scale_row = iota((2 * BLOCK, packed), 0) % BLOCK
     scale_lane = iota((2 * BLOCK, packed), 1)
@@ -438,68 +502,67 @@
     )
     scale = lax.rsqrt(own_square / depth + EPSILON)
 
-    wait_bytes(gu_recv.at[pl.ds(0, chips - 1)], recv_sem.at[10])
-    gsum[0 : 2 * BLOCK, :] = jnp.sum(gu_recv[...].astype(F32), axis=0) * scale
-    gsum[2 * BLOCK : 2 * PADB, :] = jnp.zeros((2 * PADB - 2 * BLOCK, ffe), F32)
-    gates = gsum[0:PADB, :]
-    ups = gsum[BLOCK : BLOCK + PADB, :]
-    hid[pl.ds(y, 1)] = (
-        (gates / (1.0 + jnp.exp(-gates)) * ups).astype(BF16).reshape(1, PADB, ffe)
-    )
-
-    def send_hid(k, carry):
-        other = lax.rem(y + k, chips)
-        remote(hid.at[y], hid.at[y], 11, exp=2 * other + c).start()
-        return carry
-
-    lax.fori_loop(1, chips, send_hid, 0)
-    load_down.wait()
-    swap_down.wait_recv()
     back_row = iota((groups * SEND, packed), 0)
     back_lane = iota((groups * SEND, packed), 1)
     back_slot = back_row // SEND
     back_rank = back_row % SEND
     back_source = (back_slot // per) * PADB + (back_slot % per) * CAP_E + back_rank
     back_pick = one_hot((back_rank < CAP_E) & (back_lane == back_source))
-    wait_bytes(hid.at[pl.ds(0, chips - 1)], recv_sem.at[11])
-    result = dot_t(hid[...].reshape(packed, ffe), wd[...]).astype(BF16)
-    ret_send[...] = dot(back_pick, result).astype(BF16).reshape(groups, SEND, chip)
-
-    def send_ret(k, carry):
-        other = lax.rem(g + k, groups)
-        remote(ret_send.at[other], ret_recv.at[g], 12, grp=other).start()
-        return carry
-
-    lax.fori_loop(1, groups, send_ret, 0)
+
+    for h in range(2):
+        first, size = spans[h]
+        base = 16 + 7 * h
+        for i in range(3, 7):
+            done("recv", base + i)
+        sums = gu_send[h][pl.ds(y, 1)][0].astype(F32)
+        for i in range(4):
+            sums = sums + gu_recv[h][i].astype(F32)
+        gsum[0 : 2 * BLOCK, 0:size] = sums * scale
+        gsum[2 * BLOCK : 2 * PADB, 0:size] = jnp.zeros((2 * PADB - 2 * BLOCK, size), F32)
+        gates = gsum[0:PADB, 0:size]
+        ups = gsum[BLOCK : BLOCK + PADB, 0:size]
+        hid[h][pl.ds(y, 1)] = (
+            (gates / (1.0 + jnp.exp(-gates)) * ups).astype(BF16).reshape(1, PADB, size)
+        )
+        send_each(
+            chips,
+            lambda k, h=h: remote(hid[h].at[y], hid[h].at[y], 11 - h, exp=2 * other_chip(k) + c),
+            hid[h],
+            11 - h,
+        )
+    done("load", 5)
+    done("recv", 4)
+    done("recv", 11)
+    result = dot_t(hid[0][...].reshape(packed, spans[0][1]), wd[:, 0 : spans[0][1]])
+    done("recv", 10)
+    result = result + dot_t(hid[1][...].reshape(packed, spans[1][1]), wd[:, spans[1][0] : ffe])
+    result = result.astype(BF16)
+    ret_send[...] = dot(back_pick, result).reshape(groups, SEND, chip).astype(BF16)
+
+    send_each(
+        groups,
+        lambda k: remote(
+            ret_send.at[other_group(k)], ret_recv.at[g], 12, grp=other_group(k)
+        ),
+        ret_recv,
+        12,
+    )
     ret_recv[pl.ds(g, 1)] = ret_send[pl.ds(g, 1)]
-    wait_bytes(ret_recv.at[pl.ds(0, groups - 1)], recv_sem.at[12])
-    both = dot(combine, ret_recv[...].reshape(groups * SEND, chip))
+    done("recv", 12)
+    returned = ret_recv[...].astype(F32).reshape(groups * SEND, chip).astype(BF16)
+    both = dot(combine, returned)
     expert_mix = both[0:ROWS] + both[ROWS : 2 * ROWS]
     mix_send[...] = jnp.where(c == 0, expert_mix[:, HDIM:chip], expert_mix[:, 0:HDIM])
-    mix_copy = remote(mix_send, mix_recv, 13, exp=sibling)
-    mix_copy.start()
+    send(mix_send, mix_recv, 13, exp=sibling)
     own = jnp.where(
         c == 0,
         residual[:, 0:HDIM] + expert_mix[:, 0:HDIM],
         residual[:, HDIM:chip] + expert_mix[:, HDIM:chip],
     )
-    mix_copy.wait_recv()
+    done("recv", 13)
     out_ref[...] = own + mix_recv[...]
 
-    qkv_copy.wait_send()
-    swap_gain.wait_send()
-    swap_router.wait_send()
-    swap_gu.wait_send()
-    swap_down.wait_send()
-    part_copy.wait_send()
-    mix_copy.wait_send()
-    wait_bytes(proj_recv.at[pl.ds(0, columns - 1)], send_sem.at[6])
-    wait_bytes(disp_recv.at[pl.ds(0, groups - 1)], send_sem.at[7])
-    wait_bytes(stat_recv.at[pl.ds(0, chips - 1)], send_sem.at[8])
-    wait_bytes(sq_recv.at[pl.ds(0, chips - 1)], send_sem.at[9])
-    wait_bytes(gu_recv.at[pl.ds(0, chips - 1)], send_sem.at[10])
-    wait_bytes(hid.at[pl.ds(0, chips - 1)], send_sem.at[11])
-    wait_bytes(ret_recv.at[pl.ds(0, groups - 1)], send_sem.at[12])
+    finish()
 
 
 def on_device(
@@ -527,6 +590,7 @@
     experts = w_router.shape[1]
     topk = routes.shape[3]
     chip = 2 * HDIM
+    spans = column_spans(ffe)
     keys = cap + HALF * PREV + 2 * ROWS
     vmem = pl.BlockSpec(memory_space=pltpu.VMEM)
     out = pl.pallas_call(
@@ -549,7 +613,7 @@
             pltpu.VMEM((2, 1, HDIM), F32),
             pltpu.VMEM((2, experts, HDIM), BF16),
             pltpu.VMEM((3, depth, HDIM), BF16),
-            pltpu.VMEM((HDIM, depth), BF16),
+            pltpu.VMEM((chip, depth), BF16),
             pltpu.VMEM((keys, HDIM), BF16),
             pltpu.VMEM((keys, HDIM), BF16),
             pltpu.VMEM((chip, 2 * ffe), BF16),
@@ -557,25 +621,28 @@
             pltpu.VMEM((2, ROWS, 4 * HDIM), BF16),
             pltpu.VMEM((ROWS, chip), F32),
             pltpu.VMEM((ROWS, chip), F32),
+            pltpu.VMEM((2, ROWS, HDIM), BF16),
             pltpu.VMEM((chips, ROWS, chip), BF16),
-            pltpu.VMEM((columns, ROWS, chip), BF16),
+            pltpu.VMEM((chips, ROWS, chip), BF16),
             pltpu.VMEM((ROWS, HDIM), F32),
             pltpu.VMEM((chips, ROWS, HDIM), F32),
             pltpu.VMEM((groups, SEND, chip), BF16),
             pltpu.VMEM((groups, SEND, chip), BF16),
             pltpu.VMEM((8, chips * PADB), F32),
             pltpu.VMEM((chips, 8, chips * PADB), F32),
-            pltpu.VMEM((chips, 2 * BLOCK, ffe), BF16),
-            pltpu.VMEM((chips, 2 * BLOCK, ffe), BF16),
-            pltpu.VMEM((2 * PADB, ffe), F32),
-            pltpu.VMEM((chips, PADB, ffe), BF16),
+            [pltpu.VMEM((chips, 2 * BLOCK, size), BF16) for _, size in spans],
+            [pltpu.VMEM((3, 2 * BLOCK, size), BF16) for _, size in spans],
+            [pltpu.VMEM((2, 2 * BLOCK, size), BF16) for _, size in spans],
+            [pltpu.VMEM((4, 2 * BLOCK, size), BF16) for _, size in spans],
+            pltpu.VMEM((2 * PADB, spans[0][1]), F32),
+            [pltpu.VMEM((chips, PADB, size), BF16) for _, size in spans],
             pltpu.VMEM((groups, SEND, chip), BF16),
             pltpu.VMEM((groups, SEND, chip), BF16),
             pltpu.VMEM((ROWS, HDIM), F32),
             pltpu.VMEM((ROWS, HDIM), F32),
             pltpu.SemaphoreType.DMA((14,)),
-            pltpu.SemaphoreType.DMA((14,)),
-            pltpu.SemaphoreType.DMA((14,)),
+            pltpu.SemaphoreType.DMA((30,)),
+            pltpu.SemaphoreType.DMA((30,)),
         ],
         compiler_params=pltpu.CompilerParams(
             collective_id=0, has_side_effects=True, vmem_limit_bytes=64 * 1024 * 1024

time: 72.8 us -> 65.7 us (0.902)
  Pallas kernels: 70.7 us -> 63.6 us
    pallas_call x1, Pallas kernels: 70.7 us -> 63.6 us  [on_device(): pl.pallas_call(functools.partial(kernel, groups, columns, topk), out_shap...]
where the time goes in v3:
time: 65.7 us; the launch traced here: 65.5 us
  Pallas kernels  63.6 us (97%)
  other arithmetic  1.29 us (2%)
  between operations  0.66 us (1%)
    pallas_call x1, Pallas kernels, on_device(): pl.pallas_call(functools.partial(kernel, groups, columns, topk), out_shap...  63.6 us

profile of v3, /device:TPU:1, one launch (start us, length us, event | category | flops | bytes accessed | tf_op | source)
XLA Modules:
  0.0 65.5 jit_solution(15652790930268407869)
XLA Ops:
  0.7 63.6 %layer.1 = f32[16,128]{1,0:T(8,128)} custom-call(bf16[1,4,4,2048]{3,2,1,0:T(4,128)(2,1)} %x_hbm.1, s32[1,4,4]{2,1,0:T(4,128)} %par_hbm.1, s32[1,4,4,6]{3,2,1,0:T(4,128)} %routes_hbm.1, s32[1]{0:T(128)S(6)} %copy.15.parts_hbm, f32[1,128]{1,0:T(1,128)} %bitcast.10, bf16[64,128]{1,0:T(8,128)(2,1)} %bitcast.9, bf16[3,2048,128]{2,1,0:T(8,128)(2,1)} %bitcast.6, ...), custom_call_target="tpu_custom_call" | custom-call | tf_op jit(solution)/shard_map/layer/pallas_call | solution.py:596
  64.2 1.3 %convert_element_type.3 = bf16[16,128]{1,0:T(8,128)(2,1)} convert(f32[16,128]{1,0:T(8,128)} %layer.1) | non-fusion elementwise | flops 2048 | bytes 12288 | tf_op jit(solution)/shard_map/convert_element_type | solution.py:667

commit v4 on v3

--- a/solution.py
+++ b/solution.py
@@ -47,9 +47,10 @@
     return high, (value - high.astype(F32)).astype(BF16)
 
 
-def column_spans(ffe):
-    first = (ffe // HDIM + 1) // 2 * HDIM
-    return (0, first), (first, ffe - first)
+def column_spans(ffe, chunks=4):
+    tiles = ffe // HDIM
+    sizes = [HDIM * (tiles // chunks + (h < tiles % chunks)) for h in range(chunks)]
+    return [(sum(sizes[:h]), sizes[h]) for h in range(chunks)]
 
 
 def kernel(
@@ -90,7 +91,6 @@
     qkv,
     part_send,
     part_recv,
-    att,
     proj_send,
     proj_recv,
     stat_send,
@@ -107,8 +107,6 @@
     hid,
     ret_send,
     ret_recv,
-    mix_send,
-    mix_recv,
     local_sem,
     send_sem,
     recv_sem,
@@ -158,58 +156,61 @@
         waits["recv", index] = copy.wait_recv
         waits["send", index] = copy.wait_send
 
-    def send_each(count, one, landing, index):
-        def step(k, carry):
-            one(k).start()
-            return carry
-
-        lax.fori_loop(1, count, step, 0)
-        whole = landing.at[pl.ds(0, count - 1)]
+    def track(count, landing, index):
+        whole = landing.at[pl.ds(0, count)]
         waits["recv", index] = pltpu.make_async_copy(whole, whole, recv_sem.at[index]).wait
         waits["send", index] = pltpu.make_async_copy(whole, whole, send_sem.at[index]).wait
 
+    def send_each(order, one, landing, index):
+        for k in order:
+            one(k).start()
+        track(len(order), landing, index)
+
+    deep = 8
+    wide_groups = groups // deep
+    group_order = [(i, j) for i in range(wide_groups) for j in range(deep) if i or j]
+    group_order.sort(key=lambda k: -min(k[0], wide_groups - k[0]) - min(k[1], deep - k[1]))
+    chip_order = sorted(range(1, chips), key=lambda k: -min(k, chips - k))
+
     def other_group(k):
-        return lax.rem(g + k, groups)
-
-    def other_column(k):
-        return lax.rem(e + k, columns)
+        return lax.rem(g // deep + k[0], wide_groups) * deep + lax.rem(g % deep + k[1], deep)
 
     def other_chip(k):
         return lax.rem(y + k, chips)
+
+    def to_chip(src, dst, index, offset):
+        send(src, dst, index, exp=2 * other_chip(offset + chips) + c)
 
     local(x_hbm.at[0], x_ref, 6)
     local(par_hbm, par_ref, 7)
     local(routes_hbm.at[0], routes_ref, 8)
     local(parts_hbm, parts_ref, 9)
-    local(wqkv_hbm, wqkv, 0)
+    for i in range(3):
+        local(wqkv_hbm.at[i], wqkv.at[:, pl.ds(HDIM * i, HDIM)], (0, 14, 15)[i])
     local(tk_hbm.at[0], tk_ref, 10)
     local(tv_hbm.at[0], tv_ref, 11)
     local(gain_hbm, gain.at[c], 12)
     local(wr_hbm, wr.at[c], 13)
     local(pk_hbm.at[0], kall.at[pl.ds(0, cap)], 1)
     local(pv_hbm.at[0], vall.at[pl.ds(0, cap)], 2)
-    local(wout_hbm, wout.at[own_rows], 3)
+    local(wout_hbm, wout.at[pl.ds(0, HDIM)], 3)
     local(wgu_hbm.at[c], wgu.at[own_rows], 4)
     local(wd_hbm.at[c], wd.at[own_rows], 5)
 
     barrier = pltpu.get_barrier_semaphore()
 
-    def greet_group(k, carry):
-        other = lax.rem(g + k, groups)
+    def greet(**where):
         pl.semaphore_signal(
-            barrier, inc=1, device_id={"grp": other}, device_id_type=pl.DeviceIdType.MESH
+            barrier, inc=1, device_id=where, device_id_type=pl.DeviceIdType.MESH
         )
-        return carry
-
-    def greet_column(k, carry):
-        other = lax.rem(e + k, columns)
-        pl.semaphore_signal(
-            barrier, inc=1, device_id={"exp": other}, device_id_type=pl.DeviceIdType.MESH
-        )
-        return carry
-
-    lax.fori_loop(1, groups, greet_group, 0)
-    lax.fori_loop(1, columns, greet_column, 0)
+
+    for k in group_order:
+        greet(grp=other_group(k))
+    for k in chip_order:
+        greet(exp=2 * other_chip(k) + c)
+    greet(exp=sibling)
+    for k in group_order:
+        greet(grp=other_group(k), exp=sibling)
 
     done("load", 6)
     done("load", 8)
@@ -227,14 +228,15 @@
                 (row_sub == HALF * s + b) & (row_lane == par_ref[0, s, b]), 1.0, parent_hot
             )
     done("load", 0)
-    for i in range(3):
-        qkv[0, :, HDIM * i : HDIM * (i + 1)] = dot(x16, wqkv[i]).astype(BF16)
+    done("load", 14)
+    done("load", 15)
+    qkv[0, :, 0 : 3 * HDIM] = dot(x16, wqkv[...]).astype(BF16)
     qkv[0, :, 3 * HDIM : 4 * HDIM] = parent_hot.astype(BF16)
 
-    pl.semaphore_wait(barrier, groups + columns - 2)
+    pl.semaphore_wait(barrier, 2 * groups + chips - 2)
 
     send(qkv.at[0], qkv.at[1], 0, grp=partner)
-    send(wout_hbm, wout.at[own_rows], 6, exp=sibling)
+    send(wout_hbm, wout.at[pl.ds(HDIM, HDIM)], 6, exp=sibling)
     send(gain_hbm, gain.at[c], 1, exp=sibling)
     send(wr_hbm, wr.at[c], 2, exp=sibling)
     send(wgu_hbm.at[1 - c], wgu.at[own_rows], 3, exp=sibling)
@@ -247,22 +249,6 @@
     done("load", 11)
     kall[tail_at:new_at, :] = tk_ref[...].astype(F32).reshape(HALF * PREV, HDIM).astype(BF16)
     vall[tail_at:new_at, :] = tv_ref[...].astype(F32).reshape(HALF * PREV, HDIM).astype(BF16)
-
-    width = groups * SEND
-    routes = rts[...]
-    hit = jnp.zeros((ROWS, experts), jnp.bool_)
-    expert_lane = iota((ROWS, experts), 1)
-    for k in range(topk):
-        hit = hit | (routes[:, k : k + 1] == expert_lane)
-    hits = one_hot(hit)
-    rank = dot(one_hot(iota((ROWS, ROWS), 1) < iota((ROWS, ROWS), 0)), hits)
-    spread_row = iota((experts, width), 0)
-    spread_lane = iota((experts, width), 1)
-    spread = one_hot(spread_row == 2 * (spread_lane // SEND) + c)
-    hit_wide = dot(hits, spread)
-    rank_wide = dot(rank.astype(BF16), spread)
-    slot_lane = (iota((ROWS, width), 1) % SEND).astype(F32)
-    place = jnp.where((rank_wide == slot_lane) & (hit_wide > 0.5), 1.0, 0.0)
 
     done("load", 1)
     done("load", 2)
@@ -329,54 +315,85 @@
         + weighted(tail_w, vall[tail_at:new_at, :])
         + weighted(new_w, vall[new_at:total, :])
     )
-    part_send[:, 0:HDIM] = mix[ROWS:tokens]
     lane = iota((ROWS, HDIM), 1)
-    part_send[:, HDIM : 2 * HDIM] = jnp.where(
-        lane < HDIM // 2, top[ROWS:tokens], weight_sum[ROWS:tokens]
-    )
-    send(part_send, part_recv, 5, grp=partner)
+    for h in (1, 0):
+        rows = slice(ROWS * h, ROWS * (h + 1))
+        part_send[h, :, 0:HDIM] = mix[rows]
+        part_send[h, :, HDIM : 2 * HDIM] = jnp.where(
+            lane < HDIM // 2, top[rows], weight_sum[rows]
+        )
+        if h == 1:
+            send(part_send.at[1], part_recv.at[2], 5, grp=partner, exp=sibling)
+            send(part_send.at[1], part_recv.at[0], 14, grp=partner)
+    send(part_send.at[0], part_recv.at[1], 15, exp=sibling)
+
+    width = groups * SEND
+    routes = rts[...]
+    hit = jnp.zeros((ROWS, experts), jnp.bool_)
+    expert_lane = iota((ROWS, experts), 1)
+    for k in range(topk):
+        hit = hit | (routes[:, k : k + 1] == expert_lane)
+    hits = one_hot(hit)
+    rank = dot(one_hot(iota((ROWS, ROWS), 1) < iota((ROWS, ROWS), 0)), hits)
+    spread_row = iota((experts, 2 * width), 0)
+    spread_lane = iota((experts, 2 * width), 1)
+    spread = one_hot(
+        spread_row == 2 * (spread_lane % width // SEND) + spread_lane // width
+    )
+    hit_wide = dot(hits, spread)
+    rank_wide = dot(rank.astype(BF16), spread)
+    slot_lane = (iota((ROWS, 2 * width), 1) % SEND).astype(F32)
+    place = jnp.where((rank_wide == slot_lane) & (hit_wide > 0.5), 1.0, 0.0)
+    own_place = jnp.where(c == 0, place[:, 0:width], place[:, width : 2 * width])
+
+    def joined(near_mix, near_tail, far_mix, far_tail):
+        near_top, near_sum = near_tail[:, 0:1], near_tail[:, HDIM // 2 : HDIM // 2 + 1]
+        far_top, far_sum = far_tail[:, 0:1], far_tail[:, HDIM // 2 : HDIM // 2 + 1]
+        best = jnp.maximum(near_top, far_top)
+        near_factor = jnp.exp(near_top - best)
+        far_factor = jnp.exp(far_top - best)
+        return (
+            (near_mix * near_factor + far_mix * far_factor)
+            / (near_sum * near_factor + far_sum * far_factor)
+        ).astype(BF16)
+
+    def halves(ref, index):
+        return ref[index, :, 0:HDIM], ref[index, :, HDIM : 2 * HDIM]
+
+    done("recv", 15)
+    done("recv", 14)
+    own_head = joined(*halves(part_send, 0), *halves(part_recv, 0))
     done("recv", 5)
-    far_mix = part_recv[:, 0:HDIM]
-    far_top = part_recv[:, HDIM : HDIM + 1]
-    far_sum = part_recv[:, HDIM + HDIM // 2 : HDIM + HDIM // 2 + 1]
-    near_top = top[0:ROWS]
-    best = jnp.maximum(near_top, far_top)
-    near_factor = jnp.exp(near_top - best)
-    far_factor = jnp.exp(far_top - best)
-    att[pl.ds(c, 1)] = (
-        (mix[0:ROWS] * near_factor + far_mix * far_factor)
-        / (weight_sum[0:ROWS] * near_factor + far_sum * far_factor)
-    ).astype(BF16).reshape(1, ROWS, HDIM)
-    send(att.at[c], att.at[c], 14, exp=sibling)
+    other_head = joined(*halves(part_recv, 1), *halves(part_recv, 2))
+    attention = jnp.concatenate([own_head, other_head], axis=1)
     done("load", 3)
     done("recv", 6)
-    done("recv", 14)
 
     chip = 2 * HDIM
-    proj = dot(jnp.concatenate([att[0], att[1]], axis=1), wout[...])
-    for d in range(chips):
-        proj_send[d] = proj[:, chip * d : chip * (d + 1)].astype(BF16)
-    send_each(
-        chips,
-        lambda k: remote(
-            proj_send.at[other_chip(k)], proj_recv.at[y], 15, exp=2 * other_chip(k) + c
-        ),
-        proj_recv,
-        15,
-    )
-    proj_recv[pl.ds(y, 1)] = proj_send[pl.ds(y, 1)]
-    residual = xs[:, pl.ds(pl.multiple_of(y * chip, chip), chip)]
-    done("recv", 15)
+
+    def features(at):
+        return pl.ds(pl.multiple_of(at * chip, chip), chip)
+
+    for k in chip_order:
+        at = other_chip(k)
+        proj_send[pl.ds(at, 1)] = (
+            dot(attention, wout[:, features(at)]).astype(BF16).reshape(1, ROWS, chip)
+        )
+        remote(proj_send.at[at], proj_recv.at[y], 16, exp=2 * at + c).start()
+    track(chips - 1, proj_recv, 16)
+    residual = xs[:, features(y)] + dot(attention, wout[:, features(y)])
+    proj_recv[pl.ds(y, 1)] = jnp.zeros((1, ROWS, chip), BF16)
+    done("recv", 16)
     residual = residual + jnp.sum(proj_recv[...].astype(F32), axis=0)
 
     rows_bf = residual.astype(BF16)
     outgoing = lax.dot_general(
-        place.astype(BF16), rows_bf, (((0,), (0,)), ((), ())), preferred_element_type=F32
+        own_place.astype(BF16), rows_bf, (((0,), (0,)), ((), ())), preferred_element_type=F32
     )
     disp_send[...] = outgoing.reshape(groups, SEND, chip).astype(BF16)
 
     send_each(
-        groups,
+        group_order,
         lambda k: remote(
             disp_send.at[other_group(k)], disp_recv.at[g], 7, grp=other_group(k)
         ),
@@ -398,7 +415,7 @@
     )
 
     send_each(
-        chips,
+        chip_order,
         lambda k: remote(stat_send, stat_recv.at[y], 8, exp=2 * other_chip(k) + c),
         stat_recv,
         8,
@@ -429,7 +446,7 @@
     sq_send[...] = squares
 
     send_each(
-        chips,
+        chip_order,
         lambda k: remote(sq_send, sq_recv.at[y], 9, exp=2 * other_chip(k) + c),
         sq_recv,
         9,
@@ -439,42 +456,35 @@
     up_in = (up_rows * gains).astype(BF16)
     done("load", 4)
     done("recv", 3)
-    def to_chip(src, dst, index, offset):
-        send(src, dst, index, exp=2 * lax.rem(y + offset + chips, chips) + c)
-
     def rows_of(offset):
-        return lax.rem(y + offset + chips, chips)
-
-    for h in range(2):
+        return other_chip(offset + chips)
+
+    chunks = len(spans)
+    for h in range(chunks):
         first, size = spans[h]
-        for at in range(first, first + size, chip):
-            wide = min(chip, first + size - at)
-            gate = dot(gate_in, wgu[:, at : at + wide]).reshape(chips, 2, 8, wide)
-            up = dot(up_in, wgu[:, ffe + at : ffe + at + wide]).reshape(chips, 2, 8, wide)
-            lanes = slice(at - first, at - first + wide)
-            gu_send[h][:, 0:8, lanes] = gate[:, 0].astype(BF16)
-            gu_send[h][:, 8:16, lanes] = (gate[:, 1] + up[:, 0]).astype(BF16)
-            gu_send[h][:, 16:24, lanes] = up[:, 1].astype(BF16)
-        base = 16 + 7 * h
-        far = 1 - 2 * h
-        to_chip(gu_send[h].at[rows_of(4)], gu_mid[h].at[2], base + 2, 2 * far)
+        gate = dot(gate_in, wgu[:, first : first + size]).reshape(chips, 2, 8, size)
+        up = dot(up_in, wgu[:, ffe + first : ffe + first + size]).reshape(chips, 2, 8, size)
+        gu_send[h][:, 0:8] = gate[:, 0].astype(BF16)
+        gu_send[h][:, 8:16] = (gate[:, 1] + up[:, 0]).astype(BF16)
+        gu_send[h][:, 16:24] = up[:, 1].astype(BF16)
+        base = 17 + 14 * h
+        to_chip(gu_send[h].at[rows_of(4)], gu_mid[h].at[2], base + 2, 2 - 4 * (h % 2))
         to_chip(gu_send[h].at[rows_of(3)], gu_mid[h].at[0], base, 1)
         to_chip(gu_send[h].at[rows_of(-3)], gu_mid[h].at[1], base + 1, -1)
-        to_chip(gu_send[h].at[rows_of(1)], gu_recv[h].at[0], base + 3, 1)
-        to_chip(gu_send[h].at[rows_of(-1)], gu_recv[h].at[1], base + 4, -1)
-    for h in range(2):
-        base = 16 + 7 * h
-        done("recv", base)
-        done("recv", base + 1)
-        done("recv", base + 2)
+    for h in range(chunks):
+        base = 17 + 14 * h
+        for i in range(3):
+            done("recv", base + i)
         for i in range(2):
             direction = 1 - 2 * i
             passing = gu_send[h][pl.ds(rows_of(2 * direction), 1)][0].astype(F32)
             passing = passing + gu_mid[h][i].astype(F32)
-            if i == h:
+            if i == h % 2:
                 passing = passing + gu_mid[h][2].astype(F32)
             gu_pass[h][i] = passing.astype(BF16)
             to_chip(gu_pass[h].at[i], gu_recv[h].at[2 + i], base + 5 + i, 2 * direction)
+        to_chip(gu_send[h].at[rows_of(1)], gu_recv[h].at[0], base + 3, 1)
+        to_chip(gu_send[h].at[rows_of(-1)], gu_recv[h].at[1], base + 4, -1)
 
     done("recv", 8)
     stats = jnp.sum(stat_recv[...], axis=0)
@@ -502,65 +512,71 @@
     )
     scale = lax.rsqrt(own_square / depth + EPSILON)
 
-    back_row = iota((groups * SEND, packed), 0)
-    back_lane = iota((groups * SEND, packed), 1)
-    back_slot = back_row // SEND
+    back_row = iota((groups * SEND, chips * BLOCK), 0)
+    back_lane = iota((groups * SEND, chips * BLOCK), 1)
     back_rank = back_row % SEND
-    back_source = (back_slot // per) * PADB + (back_slot % per) * CAP_E + back_rank
+    back_source = (back_row // SEND) * CAP_E + back_rank
     back_pick = one_hot((back_rank < CAP_E) & (back_lane == back_source))
 
-    for h in range(2):
+    def forward(h):
+        base = 17 + 14 * h
+        for i in range(2):
+            direction = 1 - 2 * i
+            done("recv", base + 7 + i)
+            origin_chip = rows_of(-2 * direction)
+            held = hid[h].at[origin_chip]
+            if i == h % 2:
+                to_chip(held, held, base + 13, 2 * direction)
+            to_chip(held, held, base + 11 + i, direction)
+
+    for h in range(chunks):
         first, size = spans[h]
-        base = 16 + 7 * h
+        base = 17 + 14 * h
         for i in range(3, 7):
             done("recv", base + i)
         sums = gu_send[h][pl.ds(y, 1)][0].astype(F32)
         for i in range(4):
             sums = sums + gu_recv[h][i].astype(F32)
-        gsum[0 : 2 * BLOCK, 0:size] = sums * scale
-        gsum[2 * BLOCK : 2 * PADB, 0:size] = jnp.zeros((2 * PADB - 2 * BLOCK, size), F32)
-        gates = gsum[0:PADB, 0:size]
-        ups = gsum[BLOCK : BLOCK + PADB, 0:size]
-        hid[h][pl.ds(y, 1)] = (
-            (gates / (1.0 + jnp.exp(-gates)) * ups).astype(BF16).reshape(1, PADB, size)
-        )
-        send_each(
-            chips,
-            lambda k, h=h: remote(hid[h].at[y], hid[h].at[y], 11 - h, exp=2 * other_chip(k) + c),
-            hid[h],
-            11 - h,
-        )
+        gsum[:, 0:size] = sums * scale
+        gates = gsum[0:BLOCK, 0:size]
+        ups = gsum[BLOCK : 2 * BLOCK, 0:size]
+        hidden = gates / (1.0 + jnp.exp(-gates)) * ups
+        hid[h][pl.ds(y, 1)] = hidden.reshape(1, BLOCK // HALF, HALF, size).astype(BF16)
+        offsets = (2, -2, 1, -1) if h < chunks - 1 else (2, -2, 1, -1, 3, -3, 4)
+        for i, offset in sorted(enumerate(offsets), key=lambda k: -abs(k[1])):
+            to_chip(hid[h].at[y], hid[h].at[y], base + 7 + i, offset)
+        if h == chunks - 2:
+            forward(0)
+    for h in range(1, chunks - 1):
+        forward(h)
     done("load", 5)
     done("recv", 4)
-    done("recv", 11)
-    result = dot_t(hid[0][...].reshape(packed, spans[0][1]), wd[:, 0 : spans[0][1]])
-    done("recv", 10)
-    result = result + dot_t(hid[1][...].reshape(packed, spans[1][1]), wd[:, spans[1][0] : ffe])
+    result = jnp.zeros((chips * BLOCK, chip), F32)
+    for h in range(chunks):
+        first, size = spans[h]
+        for i in range(9 if h < chunks - 1 else 7, 14):
+            done("recv", 17 + 14 * h + i)
+        rows = hid[h][...].astype(F32).reshape(chips * BLOCK, size).astype(BF16)
+        result = result + dot_t(rows, wd[:, first : first + size])
     result = result.astype(BF16)
-    ret_send[...] = dot(back_pick, result).reshape(groups, SEND, chip).astype(BF16)
-
-    send_each(
-        groups,
-        lambda k: remote(
-            ret_send.at[other_group(k)], ret_recv.at[g], 12, grp=other_group(k)
-        ),
-        ret_recv,
-        12,
-    )
-    ret_recv[pl.ds(g, 1)] = ret_send[pl.ds(g, 1)]
+    outcome = dot(back_pick, result)
+    for h in range(2):
+        ret_send[h] = outcome[:, HDIM * h : HDIM * (h + 1)].reshape(groups, SEND, HDIM).astype(BF16)
+    landing = c * groups + g
+    for k in group_order:
+        at = other_group(k)
+        remote(ret_send.at[c, at], ret_recv.at[landing], 12, grp=at).start()
+        remote(ret_send.at[1 - c, at], ret_recv.at[landing], 12, grp=at, exp=sibling).start()
+    remote(ret_send.at[1 - c, g], ret_recv.at[landing], 12, exp=sibling).start()
+    track(2 * groups - 1, ret_recv, 12)
+    ret_recv[pl.ds(landing, 1)] = ret_send[c, pl.ds(g, 1)]
+    own = jnp.where(c == 0, residual[:, 0:HDIM], residual[:, HDIM:chip])
     done("recv", 12)
-    returned = ret_recv[...].astype(F32).reshape(groups * SEND, chip).astype(BF16)
+    returned = ret_recv[...].astype(F32).reshape(2 * groups * SEND, HDIM).astype(BF16)
     both = dot(combine, returned)
-    expert_mix = both[0:ROWS] + both[ROWS : 2 * ROWS]
-    mix_send[...] = jnp.where(c == 0, expert_mix[:, HDIM:chip], expert_mix[:, 0:HDIM])
-    send(mix_send, mix_recv, 13, exp=sibling)
-    own = jnp.where(
-        c == 0,
-        residual[:, 0:HDIM] + expert_mix[:, 0:HDIM],
-        residual[:, HDIM:chip] + expert_mix[:, HDIM:chip],
-    )
-    done("recv", 13)
-    out_ref[...] = own + mix_recv[...]
+    out_ref[0] = (
+        (own + both[0:ROWS] + both[ROWS : 2 * ROWS]).reshape(STEPS, HALF, HDIM).astype(BF16)
+    )
 
     finish()
 
@@ -595,7 +611,7 @@
     vmem = pl.BlockSpec(memory_space=pltpu.VMEM)
     out = pl.pallas_call(
         functools.partial(kernel, groups, columns, topk),
-        out_shape=jax.ShapeDtypeStruct((ROWS, HDIM), F32),
+        out_shape=jax.ShapeDtypeStruct((1, STEPS, HALF, HDIM), BF16),
         in_specs=[
             pl.BlockSpec(memory_space=pltpu.HBM)
         ]
@@ -612,16 +628,15 @@
             pltpu.VMEM((ROWS, HDIM), jnp.int32),
             pltpu.VMEM((2, 1, HDIM), F32),
             pltpu.VMEM((2, experts, HDIM), BF16),
-            pltpu.VMEM((3, depth, HDIM), BF16),
+            pltpu.VMEM((depth, 3 * HDIM), BF16),
             pltpu.VMEM((chip, depth), BF16),
             pltpu.VMEM((keys, HDIM), BF16),
             pltpu.VMEM((keys, HDIM), BF16),
             pltpu.VMEM((chip, 2 * ffe), BF16),
             pltpu.VMEM((chip, ffe), BF16),
             pltpu.VMEM((2, ROWS, 4 * HDIM), BF16),
-            pltpu.VMEM((ROWS, chip), F32),
-            pltpu.VMEM((ROWS, chip), F32),
-            pltpu.VMEM((2, ROWS, HDIM), BF16),
+            pltpu.VMEM((2, ROWS, chip), F32),
+            pltpu.VMEM((3, ROWS, chip), F32),
             pltpu.VMEM((chips, ROWS, chip), BF16),
             pltpu.VMEM((chips, ROWS, chip), BF16),
             pltpu.VMEM((ROWS, HDIM), F32),
@@ -634,15 +649,13 @@
             [pltpu.VMEM((3, 2 * BLOCK, size), BF16) for _, size in spans],
             [pltpu.VMEM((2, 2 * BLOCK, size), BF16) for _, size in spans],
             [pltpu.VMEM((4, 2 * BLOCK, size), BF16) for _, size in spans],
-            pltpu.VMEM((2 * PADB, spans[0][1]), F32),
-            [pltpu.VMEM((chips, PADB, size), BF16) for _, size in spans],
-            pltpu.VMEM((groups, SEND, chip), BF16),
-            pltpu.VMEM((groups, SEND, chip), BF16),
-            pltpu.VMEM((ROWS, HDIM), F32),
-            pltpu.VMEM((ROWS, HDIM), F32),
-            pltpu.SemaphoreType.DMA((14,)),
-            pltpu.SemaphoreType.DMA((30,)),
-            pltpu.SemaphoreType.DMA((30,)),
+            pltpu.VMEM((2 * BLOCK, spans[0][1]), F32),
+            [pltpu.VMEM((chips, BLOCK // HALF, HALF, size), BF16) for _, size in spans],
+            pltpu.VMEM((2, groups, SEND, HDIM), BF16),
+            pltpu.VMEM((2 * groups, SEND, HDIM), BF16),
+            pltpu.SemaphoreType.DMA((16,)),
+            pltpu.SemaphoreType.DMA((17 + 14 * len(spans),)),
+            pltpu.SemaphoreType.DMA((17 + 14 * len(spans),)),
         ],
         compiler_params=pltpu.CompilerParams(
             collective_id=0, has_side_effects=True, vmem_limit_bytes=64 * 1024 * 1024
@@ -664,7 +677,7 @@
         w_gate_up,
         w_down,
     )
-    return out.astype(BF16).reshape(1, STEPS, HALF, HDIM)
+    return out
 
 
 def solution(mesh):

time: 65.7 us -> 63 us (0.959)
  Pallas kernels: 63.6 us -> 60.9 us
  other arithmetic: 1.29 us -> 0 us
  local copies, waits for them, and re-layouts: 0 us -> 1.28 us
    pallas_call x1, Pallas kernels: 63.6 us -> 60.9 us  [on_device(): pl.pallas_call(functools.partial(kernel, groups, columns, topk), out_shap...]
    convert_element_type x1 -> x0, other arithmetic: 1.29 us -> none  [on_device(): return out.astype(BF16).reshape(1, STEPS, HALF, HDIM)]
    unnamed x0 -> x1, local copies, waits for them, and re-layouts: none -> 1.28 us
where the time goes in v4:
time: 63 us; the launch traced here: 62.9 us
  Pallas kernels  60.9 us (97%)
  local copies, waits for them, and re-layouts  1.28 us (2%)
  between operations  0.66 us (1%)
    pallas_call x1, Pallas kernels, on_device(): pl.pallas_call(functools.partial(kernel, groups, columns, topk), out_shap...  60.9 us
    unnamed x1, local copies, waits for them, and re-layouts  1.28 us

profile of v4, /device:TPU:1, one launch (start us, length us, event | category | flops | bytes accessed | tf_op | source)
XLA Modules:
  0.0 62.9 jit_solution(17952348880801637141)
XLA Ops:
  0.7 60.9 %layer.1 = bf16[1,4,4,128]{3,2,1,0:T(4,128)(2,1)} custom-call(bf16[1,4,4,2048]{3,2,1,0:T(4,128)(2,1)} %x_hbm.1, s32[1,4,4]{2,1,0:T(4,128)} %par_hbm.1, s32[1,4,4,6]{3,2,1,0:T(4,128)} %routes_hbm.1, s32[1]{0:T(128)S(6)} %copy.16.parts_hbm, f32[1,128]{1,0:T(1,128)} %bitcast.9, bf16[64,128]{1,0:T(8,128)(2,1)} %bitcast.8, bf16[3,2048,128]{2,1,0:T(8,128)(2,1)} %bitcast.5, ...), custom_call_target="tpu_custom_call" | custom-call | tf_op jit(solution)/shard_map/layer/pallas_call | solution.py:612
  61.6 1.3 %copy.17 = bf16[1,4,4,128]{3,2,1,0:T(4,128)(2,1)} copy(bf16[1,4,4,128]{3,2,1,0:T(4,128)(2,1)} %layer.1) | data formatting | bytes 8192

commit v5 on v4

--- a/solution.py
+++ b/solution.py
@@ -47,7 +47,7 @@
     return high, (value - high.astype(F32)).astype(BF16)
 
 
-def column_spans(ffe, chunks=4):
+def column_spans(ffe, chunks=3):
     tiles = ffe // HDIM
     sizes = [HDIM * (tiles // chunks + (h < tiles % chunks)) for h in range(chunks)]
     return [(sum(sizes[:h]), sizes[h]) for h in range(chunks)]
@@ -110,6 +110,7 @@
     local_sem,
     send_sem,
     recv_sem,
+    rounds,
 ):
     chips = columns // 2
     ffe = wd.shape[1]
@@ -199,18 +200,36 @@
 
     barrier = pltpu.get_barrier_semaphore()
 
-    def greet(**where):
+    def greet(semaphore, **where):
         pl.semaphore_signal(
-            barrier, inc=1, device_id=where, device_id_type=pl.DeviceIdType.MESH
+            semaphore, inc=1, device_id=where, device_id_type=pl.DeviceIdType.MESH
         )
 
-    for k in group_order:
-        greet(grp=other_group(k))
-    for k in chip_order:
-        greet(exp=2 * other_chip(k) + c)
-    greet(exp=sibling)
-    for k in group_order:
-        greet(grp=other_group(k), exp=sibling)
+    def along_y(semaphore):
+        for k in (1, chips - 1):
+            greet(semaphore, exp=2 * other_chip(k) + c)
+
+    def along_z(semaphore):
+        for k in (1, deep - 1):
+            greet(semaphore, grp=other_group((0, k)))
+
+    def along_x(semaphore):
+        for k in (1, wide_groups - 1):
+            greet(semaphore, grp=other_group((k, 0)))
+
+    along_x(barrier)
+    along_y(barrier)
+    along_z(barrier)
+    greet(barrier, exp=sibling)
+    greet(barrier, grp=partner, exp=sibling)
+
+    def pass_word(index):
+        along_y(rounds.at[index])
+        along_z(rounds.at[3 + index])
+
+    def hear_word(index):
+        pl.semaphore_wait(rounds.at[index], 2)
+        pl.semaphore_wait(rounds.at[3 + index], 2)
 
     done("load", 6)
     done("load", 8)
@@ -233,7 +252,8 @@
     qkv[0, :, 0 : 3 * HDIM] = dot(x16, wqkv[...]).astype(BF16)
     qkv[0, :, 3 * HDIM : 4 * HDIM] = parent_hot.astype(BF16)
 
-    pl.semaphore_wait(barrier, 2 * groups + chips - 2)
+    pl.semaphore_wait(barrier, 8)
+    pass_word(0)
 
     send(qkv.at[0], qkv.at[1], 0, grp=partner)
     send(wout_hbm, wout.at[pl.ds(HDIM, HDIM)], 6, exp=sibling)
@@ -252,6 +272,8 @@
 
     done("load", 1)
     done("load", 2)
+    hear_word(0)
+    pass_word(1)
     done("recv", 0)
     for h in range(2):
         at = new_at + ROWS * h
@@ -326,6 +348,8 @@
             send(part_send.at[1], part_recv.at[2], 5, grp=partner, exp=sibling)
             send(part_send.at[1], part_recv.at[0], 14, grp=partner)
     send(part_send.at[0], part_recv.at[1], 15, exp=sibling)
+    hear_word(1)
+    pass_word(2)
 
     width = groups * SEND
     routes = rts[...]
@@ -368,6 +392,8 @@
     attention = jnp.concatenate([own_head, other_head], axis=1)
     done("load", 3)
     done("recv", 6)
+    hear_word(2)
+    along_x(rounds.at[6])
 
     chip = 2 * HDIM
 
@@ -381,9 +407,12 @@
         )
         remote(proj_send.at[at], proj_recv.at[y], 16, exp=2 * at + c).start()
     track(chips - 1, proj_recv, 16)
+    pl.semaphore_wait(rounds.at[6], 2)
+    along_x(rounds.at[7])
     residual = xs[:, features(y)] + dot(attention, wout[:, features(y)])
     proj_recv[pl.ds(y, 1)] = jnp.zeros((1, ROWS, chip), BF16)
     done("recv", 16)
+    pl.semaphore_wait(rounds.at[7], 2)
     residual = residual + jnp.sum(proj_recv[...].astype(F32), axis=0)
 
     rows_bf = residual.astype(BF16)
@@ -401,6 +430,7 @@
         7,
     )
     disp_recv[pl.ds(g, 1)] = disp_send[pl.ds(g, 1)]
+    greet(rounds.at[8], exp=sibling)
 
     done("load", 12)
     done("load", 13)
@@ -518,17 +548,6 @@
     back_source = (back_row // SEND) * CAP_E + back_rank
     back_pick = one_hot((back_rank < CAP_E) & (back_lane == back_source))
 
-    def forward(h):
-        base = 17 + 14 * h
-        for i in range(2):
-            direction = 1 - 2 * i
-            done("recv", base + 7 + i)
-            origin_chip = rows_of(-2 * direction)
-            held = hid[h].at[origin_chip]
-            if i == h % 2:
-                to_chip(held, held, base + 13, 2 * direction)
-            to_chip(held, held, base + 11 + i, direction)
-
     for h in range(chunks):
         first, size = spans[h]
         base = 17 + 14 * h
@@ -542,19 +561,14 @@
         ups = gsum[BLOCK : 2 * BLOCK, 0:size]
         hidden = gates / (1.0 + jnp.exp(-gates)) * ups
         hid[h][pl.ds(y, 1)] = hidden.reshape(1, BLOCK // HALF, HALF, size).astype(BF16)
-        offsets = (2, -2, 1, -1) if h < chunks - 1 else (2, -2, 1, -1, 3, -3, 4)
-        for i, offset in sorted(enumerate(offsets), key=lambda k: -abs(k[1])):
+        for i, offset in enumerate((4, 3, -3, 2, -2, 1, -1)):
             to_chip(hid[h].at[y], hid[h].at[y], base + 7 + i, offset)
-        if h == chunks - 2:
-            forward(0)
-    for h in range(1, chunks - 1):
-        forward(h)
     done("load", 5)
     done("recv", 4)
     result = jnp.zeros((chips * BLOCK, chip), F32)
     for h in range(chunks):
         first, size = spans[h]
-        for i in range(9 if h < chunks - 1 else 7, 14):
+        for i in range(7, 14):
             done("recv", 17 + 14 * h + i)
         rows = hid[h][...].astype(F32).reshape(chips * BLOCK, size).astype(BF16)
         result = result + dot_t(rows, wd[:, first : first + size])
@@ -563,6 +577,7 @@
     for h in range(2):
         ret_send[h] = outcome[:, HDIM * h : HDIM * (h + 1)].reshape(groups, SEND, HDIM).astype(BF16)
     landing = c * groups + g
+    pl.semaphore_wait(rounds.at[8], 1)
     for k in group_order:
         at = other_group(k)
         remote(ret_send.at[c, at], ret_recv.at[landing], 12, grp=at).start()
@@ -656,6 +671,7 @@
             pltpu.SemaphoreType.DMA((16,)),
             pltpu.SemaphoreType.DMA((17 + 14 * len(spans),)),
             pltpu.SemaphoreType.DMA((17 + 14 * len(spans),)),
+            pltpu.SemaphoreType.REGULAR((9,)),
         ],
         compiler_params=pltpu.CompilerParams(
             collective_id=0, has_side_effects=True, vmem_limit_bytes=64 * 1024 * 1024

time: 63 us -> 60.4 us (0.959)
  Pallas kernels: 60.9 us -> 58.3 us
    pallas_call x1, Pallas kernels: 60.9 us -> 58.3 us  [on_device(): pl.pallas_call(functools.partial(kernel, groups, columns, topk), out_shap...]
where the time goes in v5:
time: 60.4 us; the launch traced here: 60.2 us
  Pallas kernels  58.3 us (97%)
  local copies, waits for them, and re-layouts  1.28 us (2%)
  between operations  0.66 us (1%)
    pallas_call x1, Pallas kernels, on_device(): pl.pallas_call(functools.partial(kernel, groups, columns, topk), out_shap...  58.3 us
    unnamed x1, local copies, waits for them, and re-layouts  1.28 us

profile of v5, /device:TPU:1, one launch (start us, length us, event | category | flops | bytes accessed | tf_op | source)
XLA Modules:
  0.0 60.2 jit_solution(12932586116273187172)
XLA Ops:
  0.7 58.3 %layer.1 = bf16[1,4,4,128]{3,2,1,0:T(4,128)(2,1)} custom-call(bf16[1,4,4,2048]{3,2,1,0:T(4,128)(2,1)} %x_hbm.1, s32[1,4,4]{2,1,0:T(4,128)} %par_hbm.1, s32[1,4,4,6]{3,2,1,0:T(4,128)} %routes_hbm.1, s32[1]{0:T(128)S(6)} %copy.16.parts_hbm, f32[1,128]{1,0:T(1,128)} %bitcast.9, bf16[64,128]{1,0:T(8,128)(2,1)} %bitcast.8, bf16[3,2048,128]{2,1,0:T(8,128)(2,1)} %bitcast.5, ...), custom_call_target="tpu_custom_call" | custom-call | tf_op jit(solution)/shard_map/layer/pallas_call | solution.py:627
  59.0 1.3 %copy.17 = bf16[1,4,4,128]{3,2,1,0:T(4,128)(2,1)} copy(bf16[1,4,4,128]{3,2,1,0:T(4,128)(2,1)} %layer.1) | data formatting | bytes 8192

commit v6 on v5

--- a/solution.py
+++ b/solution.py
@@ -596,6 +596,10 @@
     finish()
 
 
+def in_hbm(value):
+    return pltpu.with_memory_space_constraint(value, pltpu.HBM)
+
+
 def on_device(
     step_inputs,
     parents,
@@ -664,7 +668,7 @@
             [pltpu.VMEM((3, 2 * BLOCK, size), BF16) for _, size in spans],
             [pltpu.VMEM((2, 2 * BLOCK, size), BF16) for _, size in spans],
             [pltpu.VMEM((4, 2 * BLOCK, size), BF16) for _, size in spans],
-            pltpu.VMEM((2 * BLOCK, spans[0][1]), F32),
+            pltpu.VMEM((2 * BLOCK, max(size for _, size in spans)), F32),
             [pltpu.VMEM((chips, BLOCK // HALF, HALF, size), BF16) for _, size in spans],
             pltpu.VMEM((2, groups, SEND, HDIM), BF16),
             pltpu.VMEM((2 * groups, SEND, HDIM), BF16),
@@ -674,24 +678,24 @@
             pltpu.SemaphoreType.REGULAR((9,)),
         ],
         compiler_params=pltpu.CompilerParams(
-            collective_id=0, has_side_effects=True, vmem_limit_bytes=64 * 1024 * 1024
+            collective_id=0, has_side_effects=True, vmem_limit_bytes=48 * 1024 * 1024
         ),
         name="layer",
     )(
-        step_inputs,
-        parents,
-        routes,
+        in_hbm(step_inputs),
+        in_hbm(parents),
+        in_hbm(routes),
         prompt_parts,
-        norm_gain.reshape(1, HDIM),
-        w_router.T,
-        jnp.transpose(w_qkv, (1, 0, 2)),
-        w_out,
-        prompt_keys,
-        prompt_values,
-        jnp.transpose(tail_keys, (0, 2, 1, 3)),
-        jnp.transpose(tail_values, (0, 2, 1, 3)),
-        w_gate_up,
-        w_down,
+        in_hbm(norm_gain.reshape(1, HDIM)),
+        in_hbm(w_router.T),
+        in_hbm(jnp.transpose(w_qkv, (1, 0, 2))),
+        in_hbm(w_out),
+        in_hbm(prompt_keys),
+        in_hbm(prompt_values),
+        in_hbm(jnp.transpose(tail_keys, (0, 2, 1, 3))),
+        in_hbm(jnp.transpose(tail_values, (0, 2, 1, 3))),
+        in_hbm(w_gate_up),
+        in_hbm(w_down),
     )
     return out
 

time: 60.4 us -> 59.1 us (0.978)
  local copies, waits for them, and re-layouts: 1.28 us -> 0.6 us
    unnamed x1, local copies, waits for them, and re-layouts: 1.28 us -> 0.6 us
where the time goes in v6:
time: 59.1 us; the launch traced here: 59 us
  Pallas kernels  57.8 us (98%)
  between operations  0.66 us (1%)
  local copies, waits for them, and re-layouts  0.6 us (1%)
    pallas_call x1, Pallas kernels, on_device(): pl.pallas_call(functools.partial(kernel, groups, columns, topk), out_shap...  57.8 us

profile of v6, /device:TPU:1, one launch (start us, length us, event | category | flops | bytes accessed | tf_op | source)
XLA Modules:
  0.0 59.0 jit_solution(5396414427961597902)
XLA Ops:
  0.7 57.8 %layer.1 = bf16[1,4,4,128]{3,2,1,0:T(4,128)(2,1)S(1)} custom-call(bf16[1,4,4,2048]{3,2,1,0:T(4,128)(2,1)} %x_hbm.1, s32[1,4,4]{2,1,0:T(4,128)} %par_hbm.1, s32[1,4,4,6]{3,2,1,0:T(4,128)} %routes_hbm.1, s32[1]{0:T(128)S(6)} %copy.16.parts_hbm, f32[1,128]{1,0:T(1,128)} %bitcast.9, bf16[64,128]{1,0:T(8,128)(2,1)} %bitcast.8, bf16[3,2048,128]{2,1,0:T(8,128)(2,1)} %bitcast.5, ...), custom_call_target="tpu_custom_call" | custom-call | tf_op jit(solution)/shard_map/layer/pallas_call | solution.py:631
  58.4 0.6 %copy.17 = bf16[1,4,4,128]{3,2,1,0:T(4,128)(2,1)} copy(bf16[1,4,4,128]{3,2,1,0:T(4,128)(2,1)S(1)} %layer.1) | data formatting | bytes 8192

commit v7 on v6

--- a/solution.py
+++ b/solution.py
@@ -470,18 +470,6 @@
     arrived = disp_recv[...].astype(F32).reshape(groups * SEND, chip).astype(BF16)
     gate_rows = dot(gate_pick, arrived)
     up_rows = dot(up_pick, arrived)
-    squares = dot_t(
-        jnp.ones((8, chip), F32), gate_rows * gate_rows, precision=lax.Precision.HIGHEST
-    )
-    sq_send[...] = squares
-
-    send_each(
-        chip_order,
-        lambda k: remote(sq_send, sq_recv.at[y], 9, exp=2 * other_chip(k) + c),
-        sq_recv,
-        9,
-    )
-    sq_recv[pl.ds(y, 1)] = squares.reshape(1, 8, packed)
     gate_in = (gate_rows * gains).astype(BF16)
     up_in = (up_rows * gains).astype(BF16)
     done("load", 4)
@@ -501,6 +489,19 @@
         to_chip(gu_send[h].at[rows_of(4)], gu_mid[h].at[2], base + 2, 2 - 4 * (h % 2))
         to_chip(gu_send[h].at[rows_of(3)], gu_mid[h].at[0], base, 1)
         to_chip(gu_send[h].at[rows_of(-3)], gu_mid[h].at[1], base + 1, -1)
+    squares = dot_t(
+        jnp.ones((8, chip), F32), gate_rows * gate_rows, precision=lax.Precision.HIGHEST
+    )
+    sq_send[...] = squares
+
+    send_each(
+        chip_order,
+        lambda k: remote(sq_send, sq_recv.at[y], 9, exp=2 * other_chip(k) + c),
+        sq_recv,
+        9,
+    )
+    sq_recv[pl.ds(y, 1)] = squares.reshape(1, 8, packed)
+
     for h in range(chunks):
         base = 17 + 14 * h
         for i in range(3):

time: 59.1 us -> 58.7 us (level)
  no operation moved by 1% of the time
where the time goes in v7:
time: 58.7 us; the launch traced here: 58.5 us
  Pallas kernels  57.3 us (98%)
  between operations  0.66 us (1%)
  local copies, waits for them, and re-layouts  0.6 us (1%)
    pallas_call x1, Pallas kernels, on_device(): pl.pallas_call(functools.partial(kernel, groups, columns, topk), out_shap...  57.3 us

profile of v7, /device:TPU:1, one launch (start us, length us, event | category | flops | bytes accessed | tf_op | source)
XLA Modules:
  0.0 58.5 jit_solution(14552023666728843657)
XLA Ops:
  0.7 57.3 %layer.1 = bf16[1,4,4,128]{3,2,1,0:T(4,128)(2,1)S(1)} custom-call(bf16[1,4,4,2048]{3,2,1,0:T(4,128)(2,1)} %x_hbm.1, s32[1,4,4]{2,1,0:T(4,128)} %par_hbm.1, s32[1,4,4,6]{3,2,1,0:T(4,128)} %routes_hbm.1, s32[1]{0:T(128)S(6)} %copy.16.parts_hbm, f32[1,128]{1,0:T(1,128)} %bitcast.9, bf16[64,128]{1,0:T(8,128)(2,1)} %bitcast.8, bf16[3,2048,128]{2,1,0:T(8,128)(2,1)} %bitcast.5, ...), custom_call_target="tpu_custom_call" | custom-call | tf_op jit(solution)/shard_map/layer/pallas_call | solution.py:632
  57.9 0.6 %copy.17 = bf16[1,4,4,128]{3,2,1,0:T(4,128)(2,1)} copy(bf16[1,4,4,128]{3,2,1,0:T(4,128)(2,1)S(1)} %layer.1) | data formatting | bytes 8192

commit v8 on v7

--- a/solution.py
+++ b/solution.py
@@ -89,6 +89,7 @@
     wgu,
     wd,
     qkv,
+    hot,
     part_send,
     part_recv,
     proj_send,
@@ -246,14 +247,14 @@
             parent_hot = jnp.where(
                 (row_sub == HALF * s + b) & (row_lane == par_ref[0, s, b]), 1.0, parent_hot
             )
+    hot[0] = parent_hot.astype(BF16)
+    pl.semaphore_wait(barrier, 8)
+    pass_word(0)
+    send(hot.at[0], hot.at[1], 10, grp=partner)
     done("load", 0)
     done("load", 14)
     done("load", 15)
     qkv[0, :, 0 : 3 * HDIM] = dot(x16, wqkv[...]).astype(BF16)
-    qkv[0, :, 3 * HDIM : 4 * HDIM] = parent_hot.astype(BF16)
-
-    pl.semaphore_wait(barrier, 8)
-    pass_word(0)
 
     send(qkv.at[0], qkv.at[1], 0, grp=partner)
     send(wout_hbm, wout.at[pl.ds(HDIM, HDIM)], 6, exp=sibling)
@@ -274,15 +275,8 @@
     done("load", 2)
     hear_word(0)
     pass_word(1)
-    done("recv", 0)
-    for h in range(2):
-        at = new_at + ROWS * h
-        kall[at : at + ROWS, :] = qkv[h, :, HDIM : 2 * HDIM]
-        vall[at : at + ROWS, :] = qkv[h, :, 2 * HDIM : 3 * HDIM]
-    query = jnp.concatenate([qkv[0, :, 0:HDIM], qkv[1, :, 0:HDIM]], axis=0)
-    parents = jnp.concatenate(
-        [qkv[0, :, 3 * HDIM : 4 * HDIM], qkv[1, :, 3 * HDIM : 4 * HDIM]], axis=0
-    )
+    done("recv", 10)
+    parents = jnp.concatenate([hot[0], hot[1]], axis=0)
     tokens = 2 * ROWS
     beam_row = iota((HDIM, tokens), 0)
     token_lane = iota((HDIM, tokens), 1)
@@ -305,6 +299,12 @@
     tail_on = dot(origin, one_hot(tail_row == HALF * half + tail_lane % HALF))
     new_on = jnp.where(iota((tokens, tokens), 0) < ROWS, path.astype(F32), 0.0)
 
+    done("recv", 0)
+    for h in range(2):
+        at = new_at + ROWS * h
+        kall[at : at + ROWS, :] = qkv[h, :, HDIM : 2 * HDIM]
+        vall[at : at + ROWS, :] = qkv[h, :, 2 * HDIM : 3 * HDIM]
+    query = jnp.concatenate([qkv[0, :, 0:HDIM], qkv[1, :, 0:HDIM]], axis=0)
     done("load", 9)
     score_scale = HDIM ** (-0.5)
     scores = dot_t(query, kall[...]) * score_scale
@@ -574,15 +574,14 @@
         rows = hid[h][...].astype(F32).reshape(chips * BLOCK, size).astype(BF16)
         result = result + dot_t(rows, wd[:, first : first + size])
     result = result.astype(BF16)
-    outcome = dot(back_pick, result)
-    for h in range(2):
-        ret_send[h] = outcome[:, HDIM * h : HDIM * (h + 1)].reshape(groups, SEND, HDIM).astype(BF16)
     landing = c * groups + g
     pl.semaphore_wait(rounds.at[8], 1)
-    for k in group_order:
-        at = other_group(k)
-        remote(ret_send.at[c, at], ret_recv.at[landing], 12, grp=at).start()
-        remote(ret_send.at[1 - c, at], ret_recv.at[landing], 12, grp=at, exp=sibling).start()
+    for h in range(2):
+        outcome = dot(back_pick, result[:, HDIM * h : HDIM * (h + 1)])
+        ret_send[h] = outcome.reshape(groups, SEND, HDIM).astype(BF16)
+        for k in group_order:
+            at = other_group(k)
+            remote(ret_send.at[h, at], ret_recv.at[landing], 12, grp=at, exp=2 * y + h).start()
     remote(ret_send.at[1 - c, g], ret_recv.at[landing], 12, exp=sibling).start()
     track(2 * groups - 1, ret_recv, 12)
     ret_recv[pl.ds(landing, 1)] = ret_send[c, pl.ds(g, 1)]
@@ -654,7 +653,8 @@
             pltpu.VMEM((keys, HDIM), BF16),
             pltpu.VMEM((chip, 2 * ffe), BF16),
             pltpu.VMEM((chip, ffe), BF16),
-            pltpu.VMEM((2, ROWS, 4 * HDIM), BF16),
+            pltpu.VMEM((2, ROWS, 3 * HDIM), BF16),
+            pltpu.VMEM((2, ROWS, HDIM), BF16),
             pltpu.VMEM((2, ROWS, chip), F32),
             pltpu.VMEM((3, ROWS, chip), F32),
             pltpu.VMEM((chips, ROWS, chip), BF16),

time: 58.7 us -> 58.5 us (level)
  no operation moved by 1% of the time
where the time goes in v8:
time: 58.5 us; the launch traced here: 58.4 us
  Pallas kernels  57.1 us (98%)
  between operations  0.66 us (1%)
  local copies, waits for them, and re-layouts  0.6 us (1%)
    pallas_call x1, Pallas kernels, on_device(): pl.pallas_call(functools.partial(kernel, groups, columns, topk), out_shap...  57.1 us

profile of v8, /device:TPU:1, one launch (start us, length us, event | category | flops | bytes accessed | tf_op | source)
XLA Modules:
  0.0 58.4 jit_solution(14697491990140296870)
XLA Ops:
  0.7 57.1 %layer.1 = bf16[1,4,4,128]{3,2,1,0:T(4,128)(2,1)S(1)} custom-call(bf16[1,4,4,2048]{3,2,1,0:T(4,128)(2,1)} %x_hbm.1, s32[1,4,4]{2,1,0:T(4,128)} %par_hbm.1, s32[1,4,4,6]{3,2,1,0:T(4,128)} %routes_hbm.1, s32[1]{0:T(128)S(6)} %copy.16.parts_hbm, f32[1,128]{1,0:T(1,128)} %bitcast.9, bf16[64,128]{1,0:T(8,128)(2,1)} %bitcast.8, bf16[3,2048,128]{2,1,0:T(8,128)(2,1)} %bitcast.5, ...), custom_call_target="tpu_custom_call" | custom-call | tf_op jit(solution)/shard_map/layer/pallas_call | solution.py:631
  57.8 0.6 %copy.17 = bf16[1,4,4,128]{3,2,1,0:T(4,128)(2,1)} copy(bf16[1,4,4,128]{3,2,1,0:T(4,128)(2,1)S(1)} %layer.1) | data formatting | bytes 8192
